TPU v7x, 32 devices: a whole 2x2x4 slice. The times are simulated.
32 devices in a mesh: gx: 2 (over x), gy: 16 (over z, y, core).
Axes of the slice: x: 2, y: 2, z: 4, core: 2. Of those that a mesh axis runs over, the one named last changes fastest.
Arguments:
- hidden_in: bfloat16 [32, 512, 768], P(('gx', 'gy')), may hold values from -6 to 6
- segment_ids: int32 [32, 512], P(('gx', 'gy')), may hold values from 0 to 511, as said below
- positions: int32 [32, 512], P(('gx', 'gy')), may hold values from 0 to 511, as said below
- token_mask: int32 [32, 512], P(('gx', 'gy')), may hold values from 0 to 1, as said below
- cotangent: bfloat16 [32, 512, 768], P(('gx', 'gy')), may hold values from -6 to 6
- qkv_weight: bfloat16 [442368], P(('gx', 'gy')), may hold values from -0.4375 to 0.4375
- out_weight: bfloat16 [589824], P(('gx', 'gy')), may hold values from -1.75 to 1.75
- up_weight: bfloat16 [589824], P(('gx', 'gy')), may hold values from -0.4375 to 0.4375
- down_weight: bfloat16 [589824], P(('gx', 'gy')), may hold values from -0.21875 to 0.21875
- biases: bfloat16 [7680], P(('gx', 'gy')), may hold values from -2.5 to 2.5
- gains: bfloat16 [1536], P(('gx', 'gy')), may hold values from 0.25 to 1.75
Outputs:
- layer_output: bfloat16 [32, 512, 768], P(('gx', 'gy'))
- input_grad: float32 [32, 512, 768], P(('gx', 'gy'))
- qkv_weight_grad: float32 [442368], P(('gx', 'gy'))
- out_weight_grad: float32 [589824], P(('gx', 'gy'))
- up_weight_grad: float32 [589824], P(('gx', 'gy'))
- down_weight_grad: float32 [589824], P(('gx', 'gy'))
- biases_grad: float32 [7680], P(('gx', 'gy'))
- gains_grad: float32 [1536], P(('gx', 'gy'))
Inputs may be any that keep to these rules, and one draw needn't show every extreme that they name: `segment_ids`: within a row segment ids start at 0 and never fall; a document is a run of tokens with one id. `positions`: positions count from 0 at the first token of each document. `token_mask`: padding stands only at the end of a row, at most 128 tokens.
All inputs are finite; a program needn't handle non-finite values.
Results may differ from a plain program's by a relative error of at most 0.012.
Values may be sent and summed in bfloat16 or wider, within the bound.
A program may use at most 128 MiB of HBM per device.

v0:
```python
import jax
import jax.numpy as jnp
from jax import lax
from jax.sharding import PartitionSpec as P

FF = 3072
HEADS = 12
GROUPS = 4


epsilon = 1e-05


def unpack(gathered, model_width):
    qkv_flat, out_flat, up_flat, down_flat, bias_flat, gain_flat = gathered
    group_width = model_width // GROUPS
    return (
        qkv_flat.reshape(GROUPS, group_width, 3 * group_width),
        out_flat.reshape(model_width, model_width),
        up_flat.reshape(GROUPS, group_width, FF // GROUPS),
        down_flat.reshape(GROUPS, FF // GROUPS, group_width),
        bias_flat.astype(jnp.float32),
        gain_flat.astype(jnp.float32),
    )


def project(inputs, weight):
    groups, width_in, width_out = weight.shape
    shaped = inputs.reshape(inputs.shape[0], groups, width_in)
    return jnp.einsum("tgi,gio->tgo", shaped, weight, preferred_element_type=jnp.float32)


def project_back(grad_rows, weight):
    result = jnp.einsum("tgo,gio->tgi", grad_rows, weight, preferred_element_type=jnp.float32)
    return result.reshape(grad_rows.shape[0], -1)


def weight_grad(inputs, grad_rows, width_in):
    shaped = inputs.reshape(inputs.shape[0], -1, width_in)
    return jnp.einsum("tgi,tgo->gio", shaped, grad_rows, preferred_element_type=jnp.float32)


def key_mask(seg_row, pos_row, valid_row):
    places = jnp.arange(seg_row.shape[0], dtype=jnp.int32)
    starts = places - pos_row
    same_doc = (seg_row[:, None] == seg_row[None, :]) & (starts[:, None] == starts[None, :])
    return same_doc & ((valid_row[None, :] == 1) | (places[:, None] == places[None, :]))


def norm_forward(summed, gain_row, shift_row):
    centred = summed - jnp.mean(summed, axis=-1, keepdims=True)
    inverse = lax.rsqrt(jnp.mean(centred * centred, axis=-1, keepdims=True) + epsilon)
    normed = centred * inverse
    return (normed * gain_row + shift_row, normed, inverse)


def norm_backward(upstream, normed, inverse, gain_row):
    scaled = upstream * gain_row
    centre = jnp.mean(scaled, axis=-1, keepdims=True)
    along = jnp.mean(scaled * normed, axis=-1, keepdims=True)
    return inverse * (scaled - centre - normed * along)


def masked_scores(queries, key_rows, seg_row, pos_row, valid_row):
    scores = (
        jnp.einsum("qhd,khd->hqk", queries, key_rows, preferred_element_type=jnp.float32) * 0.125
    )
    return jnp.where(key_mask(seg_row, pos_row, valid_row)[None], scores, -1000000000.0)


def attend_row(packed):
    queries, key_rows, value_rows, seg_row, pos_row, valid_row = packed
    scores = masked_scores(queries, key_rows, seg_row, pos_row, valid_row)
    row_max = jnp.max(scores, axis=-1, keepdims=True)
    log_total = row_max + jnp.log(jnp.sum(jnp.exp(scores - row_max), axis=-1, keepdims=True))
    probability = jnp.exp(scores - log_total).astype(jnp.bfloat16)
    context = jnp.einsum(
        "hqk,khd->qhd", probability, value_rows, preferred_element_type=jnp.float32
    )
    return (context.astype(jnp.bfloat16), log_total)


def attend_back(packed):
    queries, key_rows, value_rows, seg_row, pos_row, valid_row, log_total, context_grad = packed
    scores = masked_scores(queries, key_rows, seg_row, pos_row, valid_row)
    probability = jnp.exp(scores - log_total)
    prob_low = probability.astype(jnp.bfloat16)
    value_grad = jnp.einsum(
        "hqk,qhd->khd", prob_low, context_grad, preferred_element_type=jnp.float32
    )
    prob_grad = jnp.einsum(
        "qhd,khd->hqk", context_grad, value_rows, preferred_element_type=jnp.float32
    )
    centre = jnp.sum(probability * prob_grad, axis=-1, keepdims=True)
    score_grad = (probability * (prob_grad - centre)).astype(jnp.bfloat16) * 0.125
    query_grad = jnp.einsum(
        "hqk,khd->qhd", score_grad, key_rows, preferred_element_type=jnp.float32
    )
    key_grad = jnp.einsum("hqk,qhd->khd", score_grad, queries, preferred_element_type=jnp.float32)
    return (
        query_grad.astype(jnp.bfloat16),
        key_grad.astype(jnp.bfloat16),
        value_grad.astype(jnp.bfloat16),
    )


def gelu_exact(summed):
    return jax.nn.gelu(summed, approximate=False)


def body(
    hidden_in,
    segment_ids,
    positions,
    token_mask,
    cotangent,
    qkv_weight,
    out_weight,
    up_weight,
    down_weight,
    biases,
    gains,
):
    row_count, length, model_width = hidden_in.shape
    group_width = model_width // GROUPS
    head_dim = model_width // HEADS
    tokens = row_count * length
    head_shape = (row_count, length, HEADS, head_dim)
    shards = (qkv_weight, out_weight, up_weight, down_weight, biases, gains)
    gathered = (
        lax.all_gather(shards[0], ("gx", "gy"), axis=0, tiled=True),
        lax.all_gather(shards[1], ("gx", "gy"), axis=0, tiled=True),
        lax.all_gather(shards[2], ("gx", "gy"), axis=0, tiled=True),
        lax.all_gather(shards[3], ("gx", "gy"), axis=0, tiled=True),
        lax.all_gather(shards[4], ("gx", "gy"), axis=0, tiled=True),
        lax.all_gather(shards[5], ("gx", "gy"), axis=0, tiled=True),
    )
    qkv_matrix, out_matrix, up_matrix, down_matrix, bias_vector, gain_vector = unpack(
        gathered, model_width
    )
    offset_up = 4 * model_width
    offset_down = 4 * model_width + FF
    offset_last = 5 * model_width + FF
    inputs = hidden_in.reshape(tokens, model_width)
    projected = project(inputs, qkv_matrix)
    queries = (
        projected[:, :, :group_width].reshape(tokens, model_width) + bias_vector[:model_width]
    ).astype(jnp.bfloat16)
    key_rows = (
        projected[:, :, group_width : 2 * group_width]
        .reshape(tokens, model_width)
        .astype(jnp.bfloat16)
    )
    value_rows = (
        projected[:, :, 2 * group_width :].reshape(tokens, model_width)
        + bias_vector[model_width : 2 * model_width]
    ).astype(jnp.bfloat16)
    query_heads = queries.reshape(head_shape)
    key_heads = key_rows.reshape(head_shape)
    value_heads = value_rows.reshape(head_shape)
    context, log_total = lax.map(
        attend_row, (query_heads, key_heads, value_heads, segment_ids, positions, token_mask)
    )
    context = context.reshape(tokens, model_width)
    attended = (
        jnp.dot(context, out_matrix, preferred_element_type=jnp.float32)
        + bias_vector[2 * model_width : 3 * model_width]
    )
    first_out, first_normed, first_inverse = norm_forward(
        inputs.astype(jnp.float32) + attended,
        gain_vector[:model_width],
        bias_vector[3 * model_width : offset_up],
    )
    first_low = first_out.astype(jnp.bfloat16)
    hidden_pre = (
        project(first_low, up_matrix).reshape(tokens, FF) + bias_vector[offset_up:offset_down]
    )
    active = gelu_exact(hidden_pre).astype(jnp.bfloat16)
    branch_out = (
        project(active, down_matrix).reshape(tokens, model_width)
        + bias_vector[offset_down:offset_last]
    )
    result, second_normed, second_inverse = norm_forward(
        first_out + branch_out, gain_vector[model_width:], bias_vector[offset_last:]
    )
    output = result.astype(jnp.bfloat16).reshape(row_count, length, model_width)
    gathered = (
        lax.all_gather(shards[0], ("gx", "gy"), axis=0, tiled=True),
        lax.all_gather(shards[1], ("gx", "gy"), axis=0, tiled=True),
        lax.all_gather(shards[2], ("gx", "gy"), axis=0, tiled=True),
        lax.all_gather(shards[3], ("gx", "gy"), axis=0, tiled=True),
        lax.all_gather(shards[4], ("gx", "gy"), axis=0, tiled=True),
        lax.all_gather(shards[5], ("gx", "gy"), axis=0, tiled=True),
    )
    qkv_matrix, out_matrix, up_matrix, down_matrix, bias_vector, gain_vector = unpack(
        gathered, model_width
    )
    upstream = cotangent.reshape(tokens, model_width).astype(jnp.float32)
    second_gain_grad = jnp.sum(upstream * second_normed, axis=0)
    second_shift_grad = jnp.sum(upstream, axis=0)
    second_grad = norm_backward(upstream, second_normed, second_inverse, gain_vector[model_width:])
    branch_grad = second_grad.astype(jnp.bfloat16)
    down_bias_grad = jnp.sum(branch_grad.astype(jnp.float32), axis=0)
    branch_groups = branch_grad.reshape(tokens, GROUPS, group_width)
    down_grad = weight_grad(active, branch_groups, FF // GROUPS)
    active_grad = project_back(branch_groups, down_matrix)
    unused_value, gelu_pull = jax.vjp(gelu_exact, hidden_pre)
    hidden_grad = gelu_pull(active_grad)[0].astype(jnp.bfloat16)
    up_bias_grad = jnp.sum(hidden_grad.astype(jnp.float32), axis=0)
    hidden_groups = hidden_grad.reshape(tokens, GROUPS, FF // GROUPS)
    up_grad = weight_grad(first_low, hidden_groups, group_width)
    first_total = second_grad + project_back(hidden_groups, up_matrix)
    first_gain_grad = jnp.sum(first_total * first_normed, axis=0)
    first_shift_grad = jnp.sum(first_total, axis=0)
    residual_grad = norm_backward(
        first_total, first_normed, first_inverse, gain_vector[:model_width]
    )
    attended_grad = residual_grad.astype(jnp.bfloat16)
    out_bias_grad = jnp.sum(attended_grad.astype(jnp.float32), axis=0)
    out_grad = jnp.einsum("ti,to->io", context, attended_grad, preferred_element_type=jnp.float32)
    context_grad = jnp.einsum(
        "to,io->ti", attended_grad, out_matrix, preferred_element_type=jnp.float32
    ).astype(jnp.bfloat16)
    query_grad, key_grad, value_grad = lax.map(
        attend_back,
        (
            query_heads,
            key_heads,
            value_heads,
            segment_ids,
            positions,
            token_mask,
            log_total,
            context_grad.reshape(head_shape),
        ),
    )
    query_grad = query_grad.reshape(tokens, model_width)
    key_grad = key_grad.reshape(tokens, model_width)
    value_grad = value_grad.reshape(tokens, model_width)
    query_bias_grad = jnp.sum(query_grad.astype(jnp.float32), axis=0)
    value_bias_grad = jnp.sum(value_grad.astype(jnp.float32), axis=0)
    joined = jnp.concatenate(
        (
            query_grad.reshape(tokens, GROUPS, group_width),
            key_grad.reshape(tokens, GROUPS, group_width),
            value_grad.reshape(tokens, GROUPS, group_width),
        ),
        axis=2,
    )
    qkv_grad = weight_grad(inputs, joined, group_width)
    input_grad = residual_grad + project_back(joined, qkv_matrix)
    bias_grad = jnp.concatenate(
        (
            query_bias_grad,
            value_bias_grad,
            out_bias_grad,
            first_shift_grad,
            up_bias_grad,
            down_bias_grad,
            second_shift_grad,
        )
    )
    gain_grad = jnp.concatenate((first_gain_grad, second_gain_grad))
    owned = (
        lax.psum_scatter(qkv_grad.reshape(-1), ("gx", "gy"), scatter_dimension=0, tiled=True),
        lax.psum_scatter(out_grad.reshape(-1), ("gx", "gy"), scatter_dimension=0, tiled=True),
        lax.psum_scatter(up_grad.reshape(-1), ("gx", "gy"), scatter_dimension=0, tiled=True),
        lax.psum_scatter(down_grad.reshape(-1), ("gx", "gy"), scatter_dimension=0, tiled=True),
        lax.psum_scatter(bias_grad, ("gx", "gy"), scatter_dimension=0, tiled=True),
        lax.psum_scatter(gain_grad, ("gx", "gy"), scatter_dimension=0, tiled=True),
    )
    return (
        output,
        input_grad.reshape(row_count, length, model_width),
        owned[0],
        owned[1],
        owned[2],
        owned[3],
        owned[4],
        owned[5],
    )


def solution(mesh):
    placed = (
        P(("gx", "gy"), None, None),
        P(("gx", "gy"), None),
        P(("gx", "gy"), None),
        P(("gx", "gy"), None),
        P(("gx", "gy"), None, None),
        P(("gx", "gy")),
        P(("gx", "gy")),
        P(("gx", "gy")),
        P(("gx", "gy")),
        P(("gx", "gy")),
        P(("gx", "gy")),
    )
    return jax.shard_map(
        body,
        mesh=mesh,
        in_specs=placed,
        out_specs=(
            P(("gx", "gy"), None, None),
            P(("gx", "gy"), None, None),
            P(("gx", "gy")),
            P(("gx", "gy")),
            P(("gx", "gy")),
            P(("gx", "gy")),
            P(("gx", "gy")),
            P(("gx", "gy")),
        ),
        check_vma=False,
    )
```

profile of v0, /device:TPU:0, one launch (start us, length us, event | category | flops | bytes accessed | tf_op | source)
XLA Modules:
  0.0 496.3 jit_solution(9616885291885252749)
XLA Ops:
  10.2 49.4 %all-gather = bf16[32,1,13824]{2,1,0:T(2,128)(2,1)S(1)} all-gather(bf16[1,1,13824]{2,1,0:T(2,128)(2,1)S(1)} %reshape.334), channel_id=1, replica_groups=mesh['gx'=2,'gy'=16] {'gx','gy'}, dimensions={0}, use_global_device_ids=true | all-gather | bytes 912384 | tf_op jit(solution)/shard_map/all_gather | solution.py:131
  59.7 5.3 %reduce.4 = bf16[32,13824]{1,0:T(8,128)(2,1)S(1)} reduce(bf16[32,1,13824]{2,1,0:T(2,128)(2,1)S(1)} %all-gather, bf16[]{:T(256)} %constant.166), dimensions={1}, to_apply=%all-gather.reduce_sub_computation | reduce | bytes 1769474 | tf_op jit(solution)/shard_map/all_gather | solution.py:131
  67.0 0.8 convolution_bitcast_fusion
  68.2 1.1 slice.91
  69.8 37.6 %all-reduce.10 = (bf16[7680]{0:T(1024)(128)(2,1)S(1)}, bf16[1536]{0:T(1024)(128)(2,1)S(1)}) all-reduce(bf16[7680]{0:T(1024)(128)(2,1)S(1)} %dynamic-update-slice, bf16[1536]{0:T(1024)(128)(2,1)S(1)} %dynamic-update-slice.1), channel_id=1, replica_groups=mesh['gx'=2,'gy'=16] {'gx','gy'}, use_global_device_ids=true, to_apply=%add | all-reduce | flops 9216 | bytes 36864
  108.5 3.4 fusion.2
  111.9 2.6 exponential_reduce_fusion
  114.5 2.0 copy-done
  117.2 8.7 %convolution_convert_fusion.2 = bf16[12,64,512]{2,1,0:T(8,128)(2,1)} fusion(f32[512,12,64]{0,2,1:T(8,128)S(1)} %bitcast.176, f32[12,64]{1,0:T(8,128)S(1)} %slice.65, f32[12,512,512]{1,2,0:T(8,128)} %copy-done, f32[12,512]{1,0:T(8,128)S(1)} %log_add_fusion, pred[512,512]{0,1:T(8,128)(4,1)S(1)} %fusion.67), kind=kOutput, calls=%fused_computation.88 | convolution fusion | flops 416415744 | bytes 15232000 | tf_op jit(solution)/shard_map/while/body/eval_jaxpr/hqk,khd->qhd/dot_general | solution.py:77
  125.9 2.6 reshape.315
  128.5 2.7 fusion.104
  132.2 2.8 reshape.317
  135.0 17.5 %fusion.15 = (bf16[512,4,768]{2,0,1:T(8,128)(2,1)}, f32[512,4,768]{2,0,1:T(8,128)}, f32[4,512,768]{2,1,0:T(8,128)}) fusion(f32[4,768]{1,0:T(4,128)} %slice.74, bf16[512,4,192]{0,2,1:T(8,128)(2,1)S(1)} %bitcast.180, bf16[4,192,768]{2,1,0:T(8,128)(2,1)S(1)} %reshape.317), kind=kOutput, calls=%fused_computation.26 | convolution fusion | flops 707788800 | bytes 17707008 | tf_op jit(solution)/shard_map/tgi,gio->tgo/dot_general | solution.py:30
  152.6 28.0 %all-gather.9.cloned.1.call-done = bf16[589824]{0:T(1024)(128)(2,1)} async-done(((bf16[18432]{0:T(1024)(128)(2,1)}), bf16[589824]{0:T(1024)(128)(2,1)}) %all-gather.9.cloned.1.call-update) | async-done | bytes 1179664 | tf_op jit(solution)/shard_map/all_gather | solution.py:134
  180.6 3.6 reshape.318
  184.2 3.5 fusion.107
  187.7 1.7 copy.66
  189.4 2.0 fusion.99
  192.6 1.4 convert_reduce_fusion.2
  194.0 2.3 copy.67
  196.3 8.9 %convert_reduce_fusion = (f32[4,768]{1,0:T(4,128)S(1)}, bf16[512,4,768]{2,0,1:T(8,128)(2,1)S(1)}) fusion(f32[512,4,768]{2,0,1:T(8,128)} %get-tuple-element.94, bf16[512,4,192]{0,2,1:T(8,128)(2,1)} %bitcast.188, bf16[4,768,192]{2,1,0:T(8,128)(2,1)} %reshape.318, f32[4,512,768]{2,1,0:T(8,128)} %get-tuple-element.110, f32[4,768]{1,0:T(4,128)S(1)} %copy-done.38), kind=kOutput, calls=%fused_computation.27 | convolution fusion | flops 630715392 | bytes 17719296 | tf_op jit(solution)/shard_map/tgo,gio->tgi/dot_general | solution.py:34
  205.2 1.7 copy-done.1
  206.9 2.3 fusion.108
  209.3 3.1 copy.69
  212.3 3.7 multiply_reduce_fusion.1
  216.6 1.7 convolution_convert_fusion
  218.3 2.3 copy.70
  220.6 7.9 %fusion.70 = f32[12,512,512]{1,2,0:T(8,128)} fusion(bf16[512,12,64]{0,2,1:T(8,128)(2,1)} %bitcast.184, f32[512,12,64]{0,2,1:T(8,128)S(1)} %bitcast.177, f32[12,64]{1,0:T(8,128)S(1)} %copy-done.33), kind=kOutput, calls=%fused_computation.96 | convolution fusion | flops 403439616 | bytes 14945280 | tf_op jit(solution)/shard_map/while/body/eval_jaxpr/qhd,khd->hqk/dot_general | solution.py:91
  228.5 7.5 %convert_reduce_fusion.4 = (f32[12,64]{1,0:T(8,128)S(1)}, bf16[12,64,512]{2,1,0:T(8,128)(2,1)}) fusion(bf16[512,12,64]{0,2,1:T(8,128)(2,1)S(1)} %bitcast.185, f32[12,512,512]{1,2,0:T(8,128)} %copy-done, f32[12,512]{1,0:T(8,128)S(1)} %copy-done.35, pred[512,512]{0,1:T(8,128)(4,1)S(1)} %copy-done.23), kind=kOutput, calls=%fused_computation.70 | convolution fusion | flops 416414976 | bytes 14445568 | tf_op jit(solution)/shard_map/while/body/eval_jaxpr/hqk,qhd->khd/dot_general | solution.py:88
  236.0 3.0 fusion.110
  239.0 2.2 fusion.80
  242.3 20.2 %convert_reduce_fusion.5 = (f32[12,64]{1,0:T(8,128)S(1)}, bf16[12,64,512]{2,1,0:T(8,128)(2,1)}) fusion(bf16[512,12,64]{0,2,1:T(8,128)(2,1)S(1)} %bitcast.183, f32[12,512,512]{1,2,0:T(8,128)} %fusion.70, f32[12,512,512]{1,2,0:T(8,128)} %copy-done, f32[12,512]{1,0:T(8,128)S(1)} %copy-done.35, pred[512,512]{0,1:T(8,128)(4,1)S(1)} %copy-done.23), kind=kOutput, calls=%fused_computation.71 | convolution fusion | flops 447878912 | bytes 27028480 | tf_op jit(solution)/shard_map/while/body/eval_jaxpr/hqk,khd->qhd/dot_general | solution.py:96
  262.6 20.7 %fusion.60 = bf16[12,64,512]{2,1,0:T(8,128)(2,1)} fusion(f32[12,512,512]{1,2,0:T(8,128)} %fusion.70, f32[12,512,512]{1,2,0:T(8,128)} %copy-done, f32[12,512]{1,0:T(8,128)S(1)} %copy-done.35, pred[512,512]{0,1:T(8,128)(4,1)S(1)} %copy-done.23, f32[512,12,64]{0,2,1:T(8,128)} %bitcast.175, f32[12,64]{1,0:T(8,128)S(1)} %copy-done.31), kind=kOutput, calls=%fused_computation.86 | convolution fusion | flops 447879680 | bytes 27814912 | tf_op jit(solution)/shard_map/while/body/eval_jaxpr/hqk,qhd->khd/dot_general | solution.py:99
  283.3 4.6 reshape.328
  287.9 3.6 reshape.326
  291.5 1.6 reshape.327
  293.1 2.6 convolution_bitcast_fusion.1
  295.7 2.0 reshape.325
  297.7 1.1 copy-done.7
  299.1 3.7 fusion.68
  302.8 2.2 copy.74
  305.2 41.2 %all-reduce.8 = (f32[7680]{0:T(1024)S(1)}, f32[1536]{0:T(1024)S(1)}) all-reduce(f32[7680]{0:T(1024)S(1)} %constant_dynamic-update-slice_fusion, f32[1536]{0:T(1024)S(1)} %pad_maximum_fusion.3), channel_id=6, replica_groups=mesh['gx'=2,'gy'=16] {'gx','gy'}, use_global_device_ids=true, to_apply=%region_22.23.clone | all-reduce | flops 9216 | bytes 73728
  347.7 1.3 add_bitcast_fusion
  349.0 134.2 %all-reduce.13.cloned.1.call-done = (f32[442368]{0:T(1024)}, f32[589824]{0:T(1024)}, f32[589824]{0:T(1024)}, f32[589824]{0:T(1024)}) async-done(((f32[442368]{0:T(1024)}, f32[589824]{0:T(1024)}, f32[589824]{0:T(1024)}, f32[589824]{0:T(1024)}), (f32[442368]{0:T(1024)}, f32[589824]{0:T(1024)}, f32[589824]{0:T(1024)}, f32[589824]{0:T(1024)})) %all-reduce.13.cloned.1.call-update) | async-done | bytes 8847376
  483.1 1.5 dynamic-slice.2
  484.7 1.5 dynamic-slice.3
  486.2 1.5 dynamic-slice.4
  487.7 1.5 dynamic-slice.1
  (143 shorter events, 12.9 us)
Async XLA Ops:
  7.2 58.6 %copy-start.27 = (bf16[1,512,768]{2,1,0:T(8,128)(2,1)S(1)}, bf16[1,512,768]{2,1,0:T(8,128)(2,1)}, u32[]{:S(2)}) copy-start(bf16[1,512,768]{2,1,0:T(8,128)(2,1)} %param.11) | copy-start | bytes 2359300
  7.2 118.7 %all-gather.5.cloned.1.call-start = ((), (), s32[]{:S(2)}) async-start(), calls=%async_computation | async-start | bytes 1216512 | tf_op jit(solution)/shard_map/all_gather | solution.py:132
  7.9 124.3 %all-gather.7.cloned.1.call-start = ((), (), s32[]{:S(2)}) async-start(), calls=%async_computation.1 | async-start | bytes 1216512 | tf_op jit(solution)/shard_map/all_gather | solution.py:133
  8.7 171.9 %all-gather.9.cloned.1.call-start = ((), (), s32[]{:S(2)}) async-start(), calls=%async_computation.2 | async-start | bytes 1216512 | tf_op jit(solution)/shard_map/all_gather | solution.py:134
  9.4 473.7 %all-reduce.13.cloned.1.call-start = ((), (), s32[]{:S(2)}) async-start(), calls=%async_computation.3 | async-start | bytes 17694720
  65.8 0.9 copy-start.15
  66.1 0.9 copy-start.19
  67.8 1.5 copy-start.42
  67.8 1.7 copy-start.43
  67.8 40.2 %copy-start.40 = (s32[1,512]{1,0:T(1,128)S(1)}, s32[1,512]{1,0:T(1,128)}, u32[]{:S(2)}) copy-start(s32[1,512]{1,0:T(1,128)} %param.13) | copy-start | bytes 6148
  67.8 40.2 %copy-start.41 = (s32[1,512]{1,0:T(1,128)S(1)}, s32[1,512]{1,0:T(1,128)}, u32[]{:S(2)}) copy-start(s32[1,512]{1,0:T(1,128)} %param.14) | copy-start | bytes 6148
  67.9 40.2 %copy-start.39 = (s32[1,512]{1,0:T(1,128)S(1)}, s32[1,512]{1,0:T(1,128)}, u32[]{:S(2)}) copy-start(s32[1,512]{1,0:T(1,128)} %param.12) | copy-start | bytes 6148
  68.2 43.7 %copy-start.8 = (f32[512,4,192]{0,2,1:T(8,128)}, f32[512,4,192]{0,2,1:T(8,128)S(1)}, u32[]{:S(2)}) copy-start(f32[512,4,192]{0,2,1:T(8,128)S(1)} %get-tuple-element.95) | copy-start | bytes 4718596
  68.2 49.0 %copy-start.9 = (f32[512,4,192]{0,2,1:T(8,128)}, f32[512,4,192]{0,2,1:T(8,128)S(1)}, u32[]{:S(2)}) copy-start(f32[512,4,192]{0,2,1:T(8,128)S(1)} %get-tuple-element.96) | copy-start | bytes 4718596
  108.0 23.6 %copy-start.28 = (f32[768]{0:T(1024)}, f32[768]{0:T(1024)S(1)}, u32[]{:S(2)}) copy-start(f32[768]{0:T(1024)S(1)} %get-tuple-element.100) | copy-start | bytes 9220
  108.0 3.8 copy-start.30
  108.5 8.7 %copy-start.22 = (pred[512,512]{0,1:T(8,128)(4,1)}, pred[512,512]{0,1:T(8,128)(4,1)S(1)}, u32[]{:S(2)}) copy-start(pred[512,512]{0,1:T(8,128)(4,1)S(1)} %fusion.67) | copy-start | bytes 786436
  111.9 4.6 copy-start
  116.5 9.5 %copy-start.34 = (f32[12,512]{1,0:T(8,128)}, f32[12,512]{1,0:T(8,128)S(1)}, u32[]{:S(2)}) copy-start(f32[12,512]{1,0:T(8,128)S(1)} %log_add_fusion) | copy-start | bytes 73732
  116.5 9.4 %copy-start.32 = (f32[12,64]{1,0:T(8,128)}, f32[12,64]{1,0:T(8,128)S(1)}, u32[]{:S(2)}) copy-start(f32[12,64]{1,0:T(8,128)S(1)} %slice.65) | copy-start | bytes 9220
  128.5 3.1 copy-start.24
  132.2 20.4 %copy-start.11 = (bf16[512,768]{0,1:T(8,128)(2,1)}, bf16[512,768]{0,1:T(8,128)(2,1)S(1)}, u32[]{:S(2)}) copy-start(bf16[512,768]{0,1:T(8,128)(2,1)S(1)} %copy.64) | copy-start | bytes 2359300
  135.0 17.5 %copy-start.13 = (bf16[4,192,768]{2,1,0:T(8,128)(2,1)}, bf16[4,192,768]{2,1,0:T(8,128)(2,1)S(1)}, u32[]{:S(2)}) copy-start(bf16[4,192,768]{2,1,0:T(8,128)(2,1)S(1)} %reshape.317) | copy-start | bytes 3538948
  184.2 5.2 %copy-start.29 = (f32[768]{0:T(1024)S(1)}, f32[768]{0:T(1024)}, u32[]{:S(2)}) copy-start(f32[768]{0:T(1024)} %copy-done.28) | copy-start | bytes 9220
  184.2 5.2 %copy-start.37 = (f32[768]{0:T(1024)S(1)}, f32[768]{0:T(1024)}, u32[]{:S(2)}) copy-start(f32[768]{0:T(1024)} %get-tuple-element.99) | copy-start | bytes 9220
  189.4 2.4 copy-start.6
  191.4 4.9 copy-start.38
  196.3 10.6 %copy-start.14 = (bf16[4,192,768]{2,1,0:T(8,128)(2,1)S(1)}, bf16[4,192,768]{2,1,0:T(8,128)(2,1)}, u32[]{:S(2)}) copy-start(bf16[4,192,768]{2,1,0:T(8,128)(2,1)} %copy-done.13) | copy-start | bytes 3538948
  205.2 1.8 copy-start.1
  205.2 7.1 %copy-start.36 = (f32[768]{0:T(1024)S(1)}, f32[768]{0:T(1024)}, u32[]{:S(2)}) copy-start(f32[768]{0:T(1024)} %get-tuple-element.98) | copy-start | bytes 9220
  212.3 4.3 copy-start.25
  216.0 4.6 copy-start.33
  216.6 22.5 %copy-start.3 = (f32[512,768]{1,0:T(8,128)}, f32[512,768]{1,0:T(8,128)S(1)}, u32[]{:S(2)}) copy-start(f32[512,768]{1,0:T(8,128)S(1)} %get-tuple-element.89) | copy-start | bytes 4718596
  216.6 4.1 copy-start.10
  220.6 7.9 %copy-start.18 = (bf16[512,768]{0,1:T(8,128)(2,1)S(1)}, bf16[512,768]{0,1:T(8,128)(2,1)}, u32[]{:S(2)}) copy-start(bf16[512,768]{0,1:T(8,128)(2,1)} %copy.70) | copy-start | bytes 2359300
  220.6 7.9 %copy-start.23 = (pred[512,512]{0,1:T(8,128)(4,1)S(1)}, pred[512,512]{0,1:T(8,128)(4,1)}, u32[]{:S(2)}) copy-start(pred[512,512]{0,1:T(8,128)(4,1)} %copy-done.22) | copy-start | bytes 786436
  220.6 7.9 %copy-start.35 = (f32[12,512]{1,0:T(8,128)S(1)}, f32[12,512]{1,0:T(8,128)}, u32[]{:S(2)}) copy-start(f32[12,512]{1,0:T(8,128)} %copy-done.34) | copy-start | bytes 73732
  228.5 7.5 %copy-start.5 = (bf16[512,4,768]{2,0,1:T(8,128)(2,1)S(1)}, bf16[512,4,768]{2,0,1:T(8,128)(2,1)}, u32[]{:S(2)}) copy-start(bf16[512,4,768]{2,0,1:T(8,128)(2,1)} %get-tuple-element.93) | copy-start | bytes 9437188
  228.5 7.5 %copy-start.21 = (bf16[512,768]{0,1:T(8,128)(2,1)S(1)}, bf16[512,768]{0,1:T(8,128)(2,1)}, u32[]{:S(2)}) copy-start(bf16[512,768]{0,1:T(8,128)(2,1)} %copy.67) | copy-start | bytes 2359300
  236.0 3.0 copy-start.26
  236.0 5.2 %copy-start.2 = (bf16[512,4,768]{2,0,1:T(8,128)(2,1)S(1)}, bf16[512,4,768]{2,0,1:T(8,128)(2,1)}, u32[]{:S(2)}) copy-start(bf16[512,4,768]{2,0,1:T(8,128)(2,1)} %copy-done.1) | copy-start | bytes 9437188
  236.0 5.2 %copy-start.12 = (bf16[512,768]{0,1:T(8,128)(2,1)S(1)}, bf16[512,768]{0,1:T(8,128)(2,1)}, u32[]{:S(2)}) copy-start(bf16[512,768]{0,1:T(8,128)(2,1)} %copy-done.11) | copy-start | bytes 2359300
  241.2 1.1 copy-start.17
  242.3 20.2 %copy-start.31 = (f32[12,64]{1,0:T(8,128)S(1)}, f32[12,64]{1,0:T(8,128)}, u32[]{:S(2)}) copy-start(f32[12,64]{1,0:T(8,128)} %copy-done.30) | copy-start | bytes 9220
  287.9 5.2 %copy-start.20 = (bf16[1,512,768]{1,2,0:T(8,128)(2,1)S(1)}, bf16[1,512,768]{1,2,0:T(8,128)(2,1)}, u32[]{:S(2)}) copy-start(bf16[1,512,768]{1,2,0:T(8,128)(2,1)} %copy-done.19) | copy-start | bytes 2359300
  297.7 1.1 copy-start.7
  297.7 1.4 copy-start.16
  299.1 48.5 %copy-start.4 = (f32[512,768]{1,0:T(8,128)S(1)}, f32[512,768]{1,0:T(8,128)}, u32[]{:S(2)}) copy-start(f32[512,768]{1,0:T(8,128)} %copy-done.3) | copy-start | bytes 4718596
Sparse Core Ops, SparseCore 0:
  10.9 57.9 all-gather.4
  71.8 52.9 all-gather.6
  127.7 52.8 all-gather.8
  297.8 185.2 all-reduce.12
where the time goes:
time: 504 us; the launch traced here: 496 us
  waiting for transfers between devices  164 us (33%)
  blocking collectives  128 us (25%)
  matrix products  118 us (23%)
  local copies, waits for them, and re-layouts  51.3 us (10%)
  other arithmetic  19.2 us (4%)
  between operations  14.9 us (3%)
    unnamed x5, waiting for transfers between devices  136 us
    unnamed x2, blocking collectives  78.8 us
    all_gather x1, blocking collectives, body(): lax.all_gather(shards[0], ('gx', 'gy'), axis=0, tiled=True)  49.4 us
    all_gather x1, waiting for transfers between devices, body(): lax.all_gather(shards[3], ('gx', 'gy'), axis=0, tiled=True)  28 us
    dot_general x3, matrix products, project(): jnp.einsum('tgi,gio->tgo', shaped, weight, preferred_element_type=jnp.flo...  21.9 us
    dot_general x1, matrix products, attend_back(): jnp.einsum('hqk,qhd->khd', score_grad, queries, preferred_element_type=jn...  20.7 us
    dot_general x1, matrix products, attend_back(): jnp.einsum('hqk,khd->qhd', score_grad, key_rows, preferred_element_type=j...  20.2 us
    unnamed x106, local copies, waits for them, and re-layouts  15.1 us
  transfers between devices with their start and end apart: 4, of which 2 were waited for; matrix products, arithmetic and copies ran while one was open for 12% of the time, Pallas kernels for 0%

commit v1 on v0

v1 whole, which is shorter than its diff:
```python
import jax
import jax.numpy as jnp
from jax import lax
from jax.experimental import pallas as pl
from jax.experimental.pallas import tpu as pltpu
from jax.sharding import PartitionSpec as P

FF = 3072
HEADS = 12
GROUPS = 4
epsilon = 1e-05
f32 = jnp.float32
bf16 = jnp.bfloat16


def dot(a, b):
    return lax.dot_general(a, b, (((1,), (0,)), ((), ())), preferred_element_type=f32)

def dot_nt(a, b):
    return lax.dot_general(a, b, (((1,), (1,)), ((), ())), preferred_element_type=f32)

def dot_tn(a, b):
    return lax.dot_general(a, b, (((0,), (0,)), ((), ())), preferred_element_type=f32)

def fold(v):
    return jnp.sum(v.reshape(v.shape[0] // 8, 8, v.shape[1]), axis=0)


def stage_qkv(s):
    T, D = s.x.shape
    gw = D // GROUPS
    for pair in range(2):
        parts = []
        for g in (2 * pair, 2 * pair + 1):
            parts.append(dot(s.x[:, g * gw:(g + 1) * gw], s.wqkv[g]))
        cols = pl.ds(pair * 2 * gw, 2 * gw)
        def both(i):
            return jnp.concatenate([parts[0][:, i * gw:(i + 1) * gw], parts[1][:, i * gw:(i + 1) * gw]], axis=1)
        s.q[:, cols] = (both(0) + s.bias(0, pair * 2 * gw, 2 * gw)).astype(bf16) * jnp.asarray(0.125, bf16)
        s.k[:, cols] = both(1).astype(bf16)
        s.v[:, cols] = (both(2) + s.bias(D, pair * 2 * gw, 2 * gw)).astype(bf16)


def stage_mask(s):
    T, D = s.x.shape
    place = lax.broadcasted_iota(jnp.int32, (1, T), 1)
    code = s.seg[...] * 1024 + (place - s.pos[...])
    keyed = jnp.where(s.tok[...] == 1, code, -1)
    keyed = jnp.broadcast_to(keyed.astype(f32), (128, T)).T
    code_f = code.astype(f32)
    for c in range(T // 128):
        cols = pl.ds(c * 128, 128)
        same = keyed == code_f[:, c * 128:(c + 1) * 128]
        rows = lax.broadcasted_iota(jnp.int32, (T, 128), 0)
        lanes = lax.broadcasted_iota(jnp.int32, (T, 128), 1) + c * 128
        s.mask[:, cols] = jnp.where(same | (rows == lanes), 0.0, -1000000000.0)


def stage_attn_fwd(s, lo, hi):
    T, D = s.x.shape
    lane = lax.broadcasted_iota(jnp.int32, (1, 128), 1)
    def pair_step(pr, carry):
        cols = pl.ds(pl.multiple_of(pr * 128, 128), 128)
        q2 = s.q[:, cols]
        k2 = s.k[:, cols]
        vT = s.v[:, cols].T
        outs = []
        for h in range(2):
            keep = (lane < 64) if h == 0 else (lane >= 64)
            qm = jnp.where(keep, q2, jnp.zeros_like(q2))
            sT = dot_nt(k2, qm) + s.mask[...]
            m = jnp.max(sT, axis=0, keepdims=True)
            e = jnp.exp(sT - m)
            l = jnp.sum(e, axis=0, keepdims=True)
            p = (e * (1.0 / l)).astype(bf16)
            s.pT[2 * pr + h] = p
            outs.append(dot(vT[64 * h:64 * h + 64], p))
        cT = jnp.concatenate(outs, axis=0).astype(bf16)
        s.ctxT[pl.ds(pl.multiple_of(pr * 128, 128), 128), :] = cT
        s.ctx[:, cols] = cT.T
        return carry
    lax.fori_loop(lo, hi, pair_step, 0)


def stage_ln1(s):
    T, D = s.x.shape
    s.att[...] = dot(s.ctx[...], s.wout[...])
    R = 32
    def step(i, carry):
        rows = pl.ds(pl.multiple_of(i * R, R), R)
        u = s.x[rows, :].astype(f32) + (s.att[rows, :] + s.bias(2 * D, 0, D))
        c = u - jnp.sum(u, axis=1, keepdims=True) * (1.0 / D)
        r = lax.rsqrt(jnp.sum(c * c, axis=1, keepdims=True) * (1.0 / D) + epsilon)
        n = c * r
        s.n1[rows, :] = n
        s.r1[rows, :] = jnp.broadcast_to(r, (R, 128))
        s.first_low[rows, :] = (n * s.gain(0) + s.bias(3 * D, 0, D)).astype(bf16)
        return carry
    lax.fori_loop(0, T // R, step, 0)


def gelu_parts(z):
    phi = 0.5 * (1.0 + lax.erf(z * 0.7071067811865476))
    dens = jnp.exp(z * z * -0.5) * 0.3989422804014327
    return z * phi, phi + z * dens


def stage_ffn(s):
    T, D = s.x.shape
    gw, fg = D // GROUPS, FF // GROUPS
    R = 128
    def step(i, carry):
        rows = pl.ds(pl.multiple_of(i * R, R), R)
        for pair in range(2):
            outs = []
            for g in (2 * pair, 2 * pair + 1):
                z = dot(s.first_low[rows, g * gw:(g + 1) * gw], s.wup[g]) + s.bias(4 * D, g * fg, fg)
                act, gp = gelu_parts(z)
                act = act.astype(bf16)
                s.active[rows, g * fg:(g + 1) * fg] = act
                s.gp[rows, g * fg:(g + 1) * fg] = gp
                outs.append(dot(act, s.wdown[g]))
            s.att[rows, pair * 2 * gw:(pair + 1) * 2 * gw] = jnp.concatenate(outs, axis=1)
        return carry
    lax.fori_loop(0, T // R, step, 0)


def stage_ln2(s):
    T, D = s.x.shape
    R = 32
    for a in (s.acc_g2, s.acc_s2, s.acc_down):
        a[...] = jnp.zeros_like(a)
    def step(i, carry):
        rows = pl.ds(pl.multiple_of(i * R, R), R)
        first = s.n1[rows, :] * s.gain(0) + s.bias(3 * D, 0, D)
        u = first + (s.att[rows, :] + s.bias(4 * D + FF, 0, D))
        c = u - jnp.sum(u, axis=1, keepdims=True) * (1.0 / D)
        r = lax.rsqrt(jnp.sum(c * c, axis=1, keepdims=True) * (1.0 / D) + epsilon)
        n = c * r
        s.out[rows, :] = (n * s.gain(D) + s.bias(5 * D + FF, 0, D)).astype(bf16)
        dy = s.cot[rows, :].astype(f32)
        s.acc_g2[...] += fold(dy * n)
        s.acc_s2[...] += fold(dy)
        e = dy * s.gain(D)
        m1 = jnp.sum(e, axis=1, keepdims=True) * (1.0 / D)
        m2 = jnp.sum(e * n, axis=1, keepdims=True) * (1.0 / D)
        du = r * (e - m1 - n * m2)
        s.dsec[rows, :] = du
        dl = du.astype(bf16)
        s.douter[rows, :] = dl
        s.acc_down[...] += fold(dl.astype(f32))
        return carry
    lax.fori_loop(0, T // R, step, 0)


def stage_ffn_back(s):
    T, D = s.x.shape
    gw, fg = D // GROUPS, FF // GROUPS
    R = 128
    s.acc_up[...] = jnp.zeros_like(s.acc_up)
    def step(i, carry):
        rows = pl.ds(pl.multiple_of(i * R, R), R)
        for pair in range(2):
            outs = []
            for g in (2 * pair, 2 * pair + 1):
                da = dot_nt(s.douter[rows, g * gw:(g + 1) * gw], s.wdown[g])
                di = (da * s.gp[rows, g * fg:(g + 1) * fg]).astype(bf16)
                s.dinner[rows, g * fg:(g + 1) * fg] = di
                s.acc_up[:, g * fg:(g + 1) * fg] += fold(di.astype(f32))
                outs.append(dot_nt(di, s.wup[g]))
            s.att[rows, pair * 2 * gw:(pair + 1) * 2 * gw] = jnp.concatenate(outs, axis=1)
        return carry
    lax.fori_loop(0, T // R, step, 0)


def stage_down_grad(s, put):
    T, D = s.x.shape
    gw, fg = D // GROUPS, FF // GROUPS
    for g in range(GROUPS):
        put(g, dot_tn(s.active[:, g * fg:(g + 1) * fg], s.douter[:, g * gw:(g + 1) * gw]))


def stage_up_grad(s, put):
    T, D = s.x.shape
    gw, fg = D // GROUPS, FF // GROUPS
    for g in range(GROUPS):
        put(g, dot_tn(s.first_low[:, g * gw:(g + 1) * gw], s.dinner[:, g * fg:(g + 1) * fg]))


def stage_ln1_back(s):
    T, D = s.x.shape
    R = 32
    for a in (s.acc_g1, s.acc_s1, s.acc_out):
        a[...] = jnp.zeros_like(a)
    def step(i, carry):
        rows = pl.ds(pl.multiple_of(i * R, R), R)
        dy = s.dsec[rows, :] + s.att[rows, :]
        n = s.n1[rows, :]
        s.acc_g1[...] += fold(dy * n)
        s.acc_s1[...] += fold(dy)
        e = dy * s.gain(0)
        m1 = jnp.sum(e, axis=1, keepdims=True) * (1.0 / D)
        m2 = jnp.sum(e * n, axis=1, keepdims=True) * (1.0 / D)
        du = s.r1[rows, 0:1] * (e - m1 - n * m2)
        s.dsec[rows, :] = du
        dl = du.astype(bf16)
        s.dattn[rows, :] = dl
        s.acc_out[...] += fold(dl.astype(f32))
        return carry
    lax.fori_loop(0, T // R, step, 0)


def stage_out_grad(s, put):
    put(dot(s.ctxT[...], s.dattn[...]))
    s.dctx[...] = dot_nt(s.dattn[...], s.wout[...]).astype(bf16)


def stage_attn_back(s, lo, hi):
    T, D = s.x.shape
    lane = lax.broadcasted_iota(jnp.int32, (1, 128), 1)
    def pair_step(pr, carry):
        start = pl.multiple_of(pr * 128, 128)
        cols = pl.ds(start, 128)
        q2 = s.q[:, cols]
        v2 = s.v[:, cols]
        dc2 = s.dctx[:, cols]
        kT = s.k[:, cols].T
        prod = (s.ctxT[cols, :].astype(f32)) * (dc2.T.astype(f32))
        dk, dv, dqT = [], [], []
        for h in range(2):
            keep = (lane < 64) if h == 0 else (lane >= 64)
            qm = jnp.where(keep, q2, jnp.zeros_like(q2))
            dcm = jnp.where(keep, dc2, jnp.zeros_like(dc2))
            p = s.pT[2 * pr + h]
            delta = jnp.sum(prod[64 * h:64 * h + 64], axis=0, keepdims=True)
            dp = dot_nt(v2, dcm)
            ds = (p.astype(f32) * (dp - delta)).astype(bf16)
            dv.append(dot(p, dcm))
            dk.append(dot(ds, qm))
            dqT.append(dot(kT[64 * h:64 * h + 64], ds))
        s.dv[:, cols] = (dv[0] + dv[1]).astype(bf16)
        s.dk[:, cols] = (dk[0] + dk[1]).astype(bf16)
        s.dq[:, cols] = (jnp.concatenate(dqT, axis=0) * 0.125).astype(bf16).T
        return carry
    lax.fori_loop(lo, hi, pair_step, 0)


def stage_qkv_grad(s, put):
    T, D = s.x.shape
    gw = D // GROUPS
    for pair in range(2):
        outs = []
        for g in (2 * pair, 2 * pair + 1):
            c = slice(g * gw, (g + 1) * gw)
            joined = jnp.concatenate([s.dq[:, c], s.dk[:, c], s.dv[:, c]], axis=1)
            put(g, dot_tn(s.x[:, c], joined))
            outs.append(dot_nt(joined, s.wqkv[g]))
        cols = slice(pair * 2 * gw, (pair + 1) * 2 * gw)
        s.din[:, cols] = s.dsec[:, cols] + jnp.concatenate(outs, axis=1)


MESH = pl.DeviceIdType.MESH
ARRAYS = ("small", "qkv", "out", "up", "down")


class Names:
    pass


class Torus:
    def __init__(self, sizes):
        self.nx, gy = sizes
        self.nc = 2 if gy % 2 == 0 else 1
        self.nz = 4 if (gy // self.nc) % 4 == 0 else 1
        self.ny = gy // self.nc // self.nz
        self.count = self.nx * gy
        self.planes = [(i, j) for i in range(self.nx) for j in range(self.ny) if i or j]
        self.planes.sort(key=lambda o: -((o[0] != 0) + (o[1] != 0)))

    def locate(self):
        gy = lax.axis_index("gy")
        self.x = lax.axis_index("gx")
        self.c = gy % self.nc
        self.y = gy // self.nc % self.ny
        self.z = gy // (self.nc * self.ny)

    def device(self, x, y, z, c):
        return (x, (z * self.ny + y) * self.nc + c)

    def place(self, x, y, z, c):
        return ((c * self.nx + x) * self.ny + y) * self.nz + z

    def place_of(self, index):
        gy_size = self.nz * self.ny * self.nc
        x, gy = index // gy_size, index % gy_size
        return self.place(x, gy // self.nc % self.ny, gy // (self.nc * self.ny), gy % self.nc)

    def plane(self, offset):
        return (self.x + offset[0]) % self.nx, (self.y + offset[1]) % self.ny

    def peers(self):
        found = [self.device(self.x, self.y, (self.z + d) % self.nz, self.c) for d in range(1, self.nz)]
        for o in self.planes:
            px, py = self.plane(o)
            found.append(self.device(px, py, self.z, self.c))
        if self.nc > 1:
            found.append(self.device(self.x, self.y, self.z, 1 - self.c))
        return found


def remote(src, dst, send, recv, device):
    return pltpu.make_async_remote_copy(
        src_ref=src, dst_ref=dst, send_sem=send, recv_sem=recv, device_id=device, device_id_type=MESH
    )


class Gather:
    def __init__(self, t, own, buf, sems):
        self.t, self.own, self.buf = t, own, buf
        self.local, self.s1, self.r1, self.s2, self.r2, self.s3, self.r3 = sems

    def first_copies(self):
        t = self.t
        mine = t.place(t.x, t.y, t.z, t.c)
        return [
            remote(self.own, self.buf.at[mine], self.s1.at[d], self.r1.at[d],
                   t.device(t.x, t.y, (t.z + d) % t.nz, t.c))
            for d in range(1, t.nz)
        ]

    def local_copy(self):
        t = self.t
        return pltpu.make_async_copy(self.own, self.buf.at[t.place(t.x, t.y, t.z, t.c)], self.local.at[0])

    def second_copies(self):
        t = self.t
        part = self.buf.at[pl.ds(t.place(t.x, t.y, 0, t.c), t.nz)]
        found = []
        for k, o in enumerate(t.planes):
            px, py = t.plane(o)
            found.append(remote(part, part, self.s2.at[k], self.r2.at[k], t.device(px, py, t.z, t.c)))
        return found

    def third_copy(self, k, offset):
        t = self.t
        px, py = (t.x + t.nx - offset[0]) % t.nx, (t.y + t.ny - offset[1]) % t.ny
        part = self.buf.at[pl.ds(t.place(px, py, 0, t.c), t.nz)]
        return remote(part, part, self.s3.at[k], self.r3.at[k], t.device(t.x, t.y, t.z, 1 - t.c))

    def begin(self):
        self.local_copy().start()
        for c in self.first_copies():
            c.start()

    def spread(self):
        for c in self.first_copies():
            c.wait_recv()
        self.local_copy().wait()
        for c in self.second_copies():
            c.start()
        if self.t.nc > 1:
            self.third_copy(len(self.t.planes), (0, 0)).start()

    def share(self):
        for k, c in enumerate(self.second_copies()):
            c.wait_recv()
            if self.t.nc > 1:
                self.third_copy(k, self.t.planes[k]).start()

    def finish(self):
        t = self.t
        for c in self.first_copies() + self.second_copies():
            c.wait_send()
        if t.nc > 1:
            for k, o in enumerate(t.planes + [(0, 0)]):
                c = self.third_copy(k, o)
                c.wait_recv()
                c.wait_send()


class Scatter:
    def __init__(self, t, buf, ra, rb, rc, out, sems):
        self.t, self.buf, self.ra, self.rb, self.rc, self.out = t, buf, ra, rb, rc, out
        self.sc = ra.at[len(t.planes)]
        self.s1, self.r1, self.s2, self.r2, self.s3, self.r3 = sems

    def core_copy(self, k, offset):
        t = self.t
        px, py = t.plane(offset)
        part = self.buf.at[pl.ds(t.place(px, py, 0, 1 - t.c), t.nz)]
        return remote(part, self.ra.at[k], self.s1.at[k], self.r1.at[k], t.device(t.x, t.y, t.z, 1 - t.c))

    def plane_copy(self, k, offset):
        t = self.t
        px, py = t.plane(offset)
        return remote(self.ra.at[k], self.rb.at[k], self.s2.at[k], self.r2.at[k], t.device(px, py, t.z, t.c))

    def line_copy(self, d):
        t = self.t
        to = (t.z + d) % t.nz
        return remote(self.sc.at[to], self.rc.at[d], self.s3.at[d], self.r3.at[d], t.device(t.x, t.y, to, t.c))

    def begin(self):
        if self.t.nc > 1:
            for k, o in enumerate(self.t.planes + [(0, 0)]):
                self.core_copy(k, o).start()

    def chip_sum(self, k, offset):
        t = self.t
        px, py = t.plane(offset)
        part = self.buf[pl.ds(t.place(px, py, 0, t.c), t.nz)].astype(f32)
        if t.nc > 1:
            self.core_copy(k, offset).wait_recv()
            part = part + self.ra[k].astype(f32)
        return part

    def planes(self):
        for k, o in enumerate(self.t.planes):
            self.ra[k] = self.chip_sum(k, o).astype(self.ra.dtype)
            self.plane_copy(k, o).start()

    def line(self):
        t = self.t
        total = self.chip_sum(len(t.planes), (0, 0))
        for k, o in enumerate(t.planes):
            self.plane_copy(k, o).wait_recv()
            total = total + self.rb[k].astype(f32)
        self.sc[...] = total.astype(self.sc.dtype)
        for d in range(1, t.nz):
            self.line_copy(d).start()

    def finish(self):
        t = self.t
        total = self.sc[t.z].astype(f32)
        for d in range(1, t.nz):
            self.line_copy(d).wait_recv()
            total = total + self.rc[d].astype(f32)
        self.out[...] = total
        for d in range(1, t.nz):
            self.line_copy(d).wait_send()
        for k, o in enumerate(t.planes):
            self.plane_copy(k, o).wait_send()
        if t.nc > 1:
            for k, o in enumerate(t.planes + [(0, 0)]):
                self.core_copy(k, o).wait_send()


def joined_rows(t, buf, first, many):
    return jnp.concatenate([buf[t.place_of(first + j)].astype(f32) for j in range(many)], axis=0).astype(bf16)


def assemble(s, t, name):
    buf = s.held[name]
    if name == "small":
        nb, ng = s.small_sizes
        for d in range(t.count):
            p = t.place_of(d)
            s.bias_v[0:1, nb * d:nb * d + nb] = buf[p, 0:1, 0:nb]
            s.gain_v[0:1, ng * d:ng * d + ng] = buf[p, 1:2, 0:ng]
        return
    per = t.count // GROUPS
    for g in range(GROUPS):
        value = joined_rows(t, buf, g * per, per)
        if name == "qkv":
            s.wqkv[g] = value
        elif name == "out":
            gw = s.wout.shape[0] // GROUPS
            s.wout[g * gw:(g + 1) * gw, :] = value
        elif name == "up":
            s.wup[g] = value
        else:
            s.wdown[g] = value


def lay_out(s, t, name, g, value):
    per = t.count // GROUPS
    buf = s.held[name]
    rows = value.shape[0] // per
    for j in range(per):
        buf[t.place_of(g * per + j)] = value[rows * j:rows * j + rows].astype(bf16)


def lay_out_small(s, t):
    T, D = s.x.shape
    nb, ng = s.small_sizes
    def rs(v):
        return jnp.sum(v, axis=0, keepdims=True)
    s.bias_v[:, 0:D] = rs(s.dq[...].astype(f32))
    s.bias_v[:, D:2 * D] = rs(s.dv[...].astype(f32))
    s.bias_v[:, 2 * D:3 * D] = rs(s.acc_out[...])
    s.bias_v[:, 3 * D:4 * D] = rs(s.acc_s1[...])
    s.bias_v[:, 4 * D:4 * D + FF] = rs(s.acc_up[...])
    s.bias_v[:, 4 * D + FF:5 * D + FF] = rs(s.acc_down[...])
    s.bias_v[:, 5 * D + FF:] = rs(s.acc_s2[...])
    s.gain_v[:, 0:D] = rs(s.acc_g1[...])
    s.gain_v[:, D:] = rs(s.acc_g2[...])
    buf = s.held["small"]
    for d in range(t.count):
        p = t.place_of(d)
        buf[p, 0:1, 0:nb] = s.bias_v[0:1, nb * d:nb * d + nb]
        buf[p, 1:2, 0:ng] = s.gain_v[0:1, ng * d:ng * d + ng]


def layer_kernel(names, t, small_sizes, *refs):
    s = Names()
    for n, r in zip(names, refs, strict=True):
        setattr(s, n, r)
    D = s.x.shape[1]
    s.small_sizes = small_sizes
    s.bias = lambda base, off, w: s.bias_v[0:1, base + off:base + off + w]
    s.gain = lambda base: s.gain_v[0:1, base:base + D]
    s.held = {n: getattr(s, "held_" + n) for n in ARRAYS}
    t.locate()

    barrier = pltpu.get_barrier_semaphore()
    peers = t.peers()
    for peer in peers:
        pl.semaphore_signal(barrier, inc=1, device_id=peer, device_id_type=MESH)
    pl.semaphore_wait(barrier, len(peers))

    gather, scatter = {}, {}
    for i, n in enumerate(ARRAYS):
        gather[n] = Gather(t, getattr(s, "in_" + n), s.held[n],
                           [getattr(s, "g_" + k).at[i] for k in ("local", "s1", "r1", "s2", "r2", "s3", "r3")])
        scatter[n] = Scatter(t, s.held[n], *[getattr(s, k + "_" + n) for k in ("ra", "rb", "rc", "grad")],
                             [getattr(s, "h_" + k).at[i] for k in ("s1", "r1", "s2", "r2", "s3", "r3")])

    gather["small"].begin()
    gather["qkv"].begin()
    stage_mask(s)
    gather["small"].spread()
    gather["qkv"].spread()
    gather["out"].begin()
    gather["small"].share()
    gather["qkv"].share()
    gather["out"].spread()
    gather["up"].begin()
    gather["small"].finish()
    gather["qkv"].finish()
    assemble(s, t, "small")
    assemble(s, t, "qkv")
    stage_qkv(s)
    gather["up"].spread()
    gather["down"].begin()
    gather["out"].share()
    stage_attn_fwd(s, 0, 2)
    gather["down"].spread()
    stage_attn_fwd(s, 2, 4)
    gather["up"].share()
    stage_attn_fwd(s, 4, 6)
    gather["down"].share()
    gather["out"].finish()
    assemble(s, t, "out")
    stage_ln1(s)
    gather["up"].finish()
    gather["down"].finish()
    assemble(s, t, "up")
    assemble(s, t, "down")
    stage_ffn(s)
    stage_ln2(s)
    stage_down_grad(s, lambda g, v: lay_out(s, t, "down", g, v))
    scatter["down"].begin()
    stage_ffn_back(s)
    scatter["down"].planes()
    stage_up_grad(s, lambda g, v: lay_out(s, t, "up", g, v))
    scatter["up"].begin()
    stage_ln1_back(s)
    def put_out(v):
        gw = D // GROUPS
        for g in range(GROUPS):
            lay_out(s, t, "out", g, v[g * gw:(g + 1) * gw])
    scatter["up"].planes()
    stage_out_grad(s, put_out)
    scatter["out"].begin()
    stage_attn_back(s, 0, 2)
    scatter["out"].planes()
    scatter["down"].line()
    stage_attn_back(s, 2, 4)
    scatter["up"].line()
    scatter["down"].finish()
    stage_attn_back(s, 4, 6)
    scatter["out"].line()
    scatter["up"].finish()
    stage_qkv_grad(s, lambda g, v: lay_out(s, t, "qkv", g, v))
    scatter["qkv"].begin()
    lay_out_small(s, t)
    scatter["small"].begin()
    scatter["qkv"].planes()
    scatter["small"].planes()
    scatter["out"].finish()
    scatter["qkv"].line()
    scatter["small"].line()
    scatter["qkv"].finish()
    scatter["small"].finish()


def body(sizes, hidden_in, segment_ids, positions, token_mask, cotangent, qkv_weight, out_weight, up_weight, down_weight, biases, gains):
    rows, T, D = hidden_in.shape
    assert rows == 1
    gw = D // GROUPS
    t = Torus(sizes)
    nb, ng = biases.shape[0], gains.shape[0]
    depth = D // t.count
    blocks = {
        "small": ((8, 256), f32),
        "qkv": ((depth, 3 * gw), bf16),
        "out": ((depth, D), bf16),
        "up": ((depth, FF // GROUPS), bf16),
        "down": ((FF // t.count, gw), bf16),
    }
    small = jnp.concatenate([
        jnp.pad(biases.astype(f32), (0, 256 - nb))[None],
        jnp.pad(gains.astype(f32), (0, 256 - ng))[None],
        jnp.zeros((6, 256), f32),
    ], axis=0)
    inputs = {
        "x": hidden_in[0], "seg": segment_ids, "pos": positions, "tok": token_mask, "cot": cotangent[0],
        "in_small": small,
        "in_qkv": qkv_weight.reshape(blocks["qkv"][0]),
        "in_out": out_weight.reshape(blocks["out"][0]),
        "in_up": up_weight.reshape(blocks["up"][0]),
        "in_down": down_weight.reshape(blocks["down"][0]),
    }
    outputs = {"out": ((T, D), bf16), "din": ((T, D), f32)}
    for n in ARRAYS:
        outputs["grad_" + n] = (blocks[n][0], f32)
    scratch = dict(
        mask=((T, T), f32), q=((T, D), bf16), k=((T, D), bf16), v=((T, D), bf16), pT=((HEADS, T, T), bf16),
        ctx=((T, D), bf16), ctxT=((D, T), bf16), att=((T, D), f32), n1=((T, D), f32), r1=((T, 128), f32),
        first_low=((T, D), bf16), active=((T, FF), bf16), gp=((T, FF), f32), dsec=((T, D), f32),
        douter=((T, D), bf16), dinner=((T, FF), bf16), dattn=((T, D), bf16), dctx=((T, D), bf16),
        dq=((T, D), bf16), dk=((T, D), bf16), dv=((T, D), bf16),
        acc_g2=((8, D), f32), acc_s2=((8, D), f32), acc_down=((8, D), f32), acc_up=((8, FF), f32),
        acc_g1=((8, D), f32), acc_s1=((8, D), f32), acc_out=((8, D), f32),
        bias_v=((1, nb * t.count), f32), gain_v=((1, ng * t.count), f32),
        wqkv=((GROUPS, gw, 3 * gw), bf16), wout=((D, D), bf16),
        wup=((GROUPS, gw, FF // GROUPS), bf16), wdown=((GROUPS, FF // GROUPS, gw), bf16),
    )
    np_ = len(t.planes)
    for n in ARRAYS:
        shape, kind = blocks[n]
        scratch["held_" + n] = ((t.count,) + shape, kind)
        scratch["ra_" + n] = ((np_ + 1, t.nz) + shape, kind)
        scratch["rb_" + n] = ((np_, t.nz) + shape, kind)
        scratch["rc_" + n] = ((t.nz,) + shape, kind)
    shapes = [pltpu.VMEM(*scratch[n]) for n in scratch]
    sems = dict(g_local=1, g_s1=t.nz, g_r1=t.nz, g_s2=np_, g_r2=np_, g_s3=np_ + 1, g_r3=np_ + 1,
                h_s1=np_ + 1, h_r1=np_ + 1, h_s2=np_, h_r2=np_, h_s3=t.nz, h_r3=t.nz)
    shapes += [pltpu.SemaphoreType.DMA((len(ARRAYS), sems[n])) for n in sems]
    names = list(inputs) + list(outputs) + list(scratch) + list(sems)
    vm = pl.BlockSpec(memory_space=pltpu.VMEM)
    found = pl.pallas_call(
        lambda *refs: layer_kernel(names, t, (nb, ng), *refs),
        out_shape=[jax.ShapeDtypeStruct(*outputs[n]) for n in outputs],
        in_specs=[vm] * len(inputs),
        out_specs=[vm] * len(outputs),
        scratch_shapes=shapes,
        compiler_params=pltpu.CompilerParams(
            collective_id=0, has_side_effects=True, vmem_limit_bytes=67043328
        ),
        name="layer",
    )(*inputs.values())
    o = dict(zip(outputs, found))
    return (
        o["out"][None], o["din"][None], o["grad_qkv"].reshape(-1), o["grad_out"].reshape(-1), o["grad_up"].reshape(-1),
        o["grad_down"].reshape(-1), o["grad_small"][0, :nb], o["grad_small"][1, :ng],
    )


def solution(mesh):
    whole = P(("gx", "gy"))
    rows2 = P(("gx", "gy"), None)
    rows3 = P(("gx", "gy"), None, None)
    sizes = (mesh.shape["gx"], mesh.shape["gy"])
    return jax.shard_map(
        lambda *args: body(sizes, *args),
        mesh=mesh,
        in_specs=(rows3, rows2, rows2, rows2, rows3) + (whole,) * 6,
        out_specs=(rows3, rows3) + (whole,) * 6,
        check_vma=False,
    )
```

time: 504 us -> 124 us (0.25); the launches traced: 496 us -> 123 us
  waiting for transfers between devices: 164 us -> 0 us
  blocking collectives: 128 us -> 0 us
  matrix products: 118 us -> 0 us
  Pallas kernels: 0 us -> 103 us
  local copies, waits for them, and re-layouts: 51.3 us -> 17.9 us
  other arithmetic: 19.2 us -> 1.99 us
  between operations: 14.9 us -> 0.66 us
    unnamed x5 -> x0, waiting for transfers between devices: 136 us -> none
    dot_general x18 -> x0, matrix products: 118 us -> none  [the longest x3 21.9 us: project(): jnp.einsum('tgi,gio->tgo', shaped, weight, preferred_element_type=jnp.flo...]
    pallas_call x0 -> x1, Pallas kernels: none -> 103 us  [body(): pl.pallas_call(lambda *refs: layer_kernel(names, t, (nb, ng), *refs), out...]
    unnamed x2 -> x0, blocking collectives: 78.8 us -> none
    all_gather x1 -> x0, blocking collectives: 49.4 us -> none  [body(): lax.all_gather(shards[0], ('gx', 'gy'), axis=0, tiled=True)]
    all_gather x3 -> x0, waiting for transfers between devices: 28 us -> none  [the longest x1 28 us: body(): lax.all_gather(shards[3], ('gx', 'gy'), axis=0, tiled=True)]
    reshape x11 -> x8, local copies, waits for them, and re-layouts: 28.4 us -> 12 us  [the longest x1 1.62 us: body(): o['grad_down'].reshape(-1)]
    unnamed x106 -> x4, local copies, waits for them, and re-layouts: 15.1 us -> 3.21 us
  transfers between devices with their start and end apart: 4 -> 0, of which waited for: 2 -> 0; matrix products, arithmetic and copies ran while one was open for 12% -> 0% of each run, Pallas kernels for 0% -> 0%
where the time goes in v1:
time: 124 us; the launch traced here: 123 us
  Pallas kernels  103 us (83%)
  local copies, waits for them, and re-layouts  17.9 us (14%)
  other arithmetic  1.99 us (2%)
    pallas_call x1, Pallas kernels, body(): pl.pallas_call(lambda *refs: layer_kernel(names, t, (nb, ng), *refs), out...  103 us
    unnamed x4, local copies, waits for them, and re-layouts  3.21 us

profile of v1, /device:TPU:0, one launch (start us, length us, event | category | flops | bytes accessed | tf_op | source)
XLA Modules:
  0.0 123.3 jit_solution(2541499990271034579)
XLA Ops:
  0.6 1.5 %reshape.43.refs_9_ = bf16[96,192]{1,0:T(8,128)(2,1)} reshape(bf16[18432]{0:T(1024)(128)(2,1)} %param.19) | data formatting | bytes 73728 | tf_op jit(solution)/shard_map/reshape | solution.py:622
  2.1 1.4 %reshape.41.refs_7_ = bf16[24,768]{1,0:T(8,128)(2,1)} reshape(bf16[18432]{0:T(1024)(128)(2,1)} %param.17) | data formatting | bytes 73728 | tf_op jit(solution)/shard_map/reshape | solution.py:620
  3.6 1.4 %reshape.42.refs_8_ = bf16[24,768]{1,0:T(8,128)(2,1)} reshape(bf16[18432]{0:T(1024)(128)(2,1)} %param.18) | data formatting | bytes 73728 | tf_op jit(solution)/shard_map/reshape | solution.py:621
  5.0 1.5 %reshape.40.refs_6_ = bf16[24,576]{1,0:T(8,128)(2,1)} reshape(bf16[13824]{0:T(1024)(128)(2,1)} %param.16) | data formatting | bytes 55296 | tf_op jit(solution)/shard_map/reshape | solution.py:619
  6.4 0.7 pad_convert_fusion.1
  7.1 0.7 pad_convert_fusion
  7.8 0.1 pad.14.clone
  7.8 0.7 maximum_maximum_fusion.refs_5_
  8.5 102.7 %layer.1 = (bf16[512,768]{1,0:T(8,128)(2,1)}, f32[512,768]{1,0:T(8,128)}, f32[8,256]{1,0:T(8,128)}, f32[24,576]{1,0:T(8,128)}, f32[24,768]{1,0:T(8,128)}, /*index=5*/f32[24,768]{1,0:T(8,128)}, f32[96,192]{1,0:T(8,128)}) custom-call(bf16[512,768]{1,0:T(8,128)(2,1)} %bitcast.10, s32[1,512]{1,0:T(1,128)} %refs_1_.1, s32[1,512]{1,0:T(1,128)} %refs_2_.1, ...), custom_call_target="tpu_custom_call" | custom-call | tf_op jit(solution)/shard_map/layer/pallas_call | solution.py:652
  111.3 0.0 copy-start
  111.3 1.4 %slice.6 = f32[1,240]{1,0:T(1,128)} slice(f32[8,256]{1,0:T(8,128)} %get-tuple-element.21), slice={[0:1], [0:240]} | slice | bytes 1920 | tf_op jit(solution)/shard_map/slice | solution.py:666
  112.6 1.2 slice_bitcast_fusion
  113.8 1.5 %reshape.45 = f32[18432]{0:T(1024)} reshape(f32[24,768]{1,0:T(8,128)} %get-tuple-element.18) | data formatting | bytes 147456 | tf_op jit(solution)/shard_map/reshape | solution.py:665
  115.4 1.5 %reshape.46 = f32[18432]{0:T(1024)} reshape(f32[24,768]{1,0:T(8,128)} %get-tuple-element.19) | data formatting | bytes 147456 | tf_op jit(solution)/shard_map/reshape | solution.py:665
  116.9 1.6 %reshape.47 = f32[18432]{0:T(1024)} reshape(f32[96,192]{1,0:T(8,128)} %get-tuple-element.20) | data formatting | bytes 147456 | tf_op jit(solution)/shard_map/reshape | solution.py:666
  118.5 1.5 %reshape.44 = f32[13824]{0:T(1024)} reshape(f32[24,576]{1,0:T(8,128)} %get-tuple-element.17) | data formatting | bytes 110592 | tf_op jit(solution)/shard_map/reshape | solution.py:665
  120.0 2.1 %copy.21 = bf16[1,512,768]{2,1,0:T(8,128)(2,1)} copy(bf16[1,512,768]{2,1,0:T(8,128)(2,1)} %bitcast.12) | data formatting | bytes 1572864
  122.1 0.0 copy-done
  122.1 1.1 copy.22
  (1 shorter events, 0.0 us)
Async XLA Ops:
  111.3 10.9 %copy-start = (f32[512,768]{1,0:T(8,128)S(1)}, f32[512,768]{1,0:T(8,128)}, u32[]{:S(2)}) copy-start(f32[512,768]{1,0:T(8,128)} %get-tuple-element.16) | copy-start | bytes 4718596

commit v2 on v1

v2 whole, which is shorter than its diff:
```python
import jax
import jax.numpy as jnp
from jax import lax
from jax.experimental import pallas as pl
from jax.experimental.pallas import tpu as pltpu
from jax.sharding import PartitionSpec as P

FF = 3072
HEADS = 12
GROUPS = 4
epsilon = 1e-05
f32 = jnp.float32
bf16 = jnp.bfloat16


def dot(a, b):
    return lax.dot_general(a, b, (((1,), (0,)), ((), ())), preferred_element_type=f32)

def dot_nt(a, b):
    return lax.dot_general(a, b, (((1,), (1,)), ((), ())), preferred_element_type=f32)

def dot_tn(a, b):
    return lax.dot_general(a, b, (((0,), (0,)), ((), ())), preferred_element_type=f32)

def fold(v):
    return jnp.sum(v.reshape(v.shape[0] // 8, 8, v.shape[1]), axis=0)


def stage_qkv(s, half):
    T, D = s.x.shape
    gw = D // GROUPS
    cols = pl.ds(pl.multiple_of(half * 2 * gw, 128), 2 * gw)
    value_cols = pl.ds(pl.multiple_of(half * 2 * gw + D, 128), 2 * gw)
    xh = s.x[:, cols]
    parts = [dot(xh[:, i * gw:(i + 1) * gw], s.wqkv[2 * half + i]) for i in range(2)]
    def both(i):
        return jnp.concatenate([parts[0][:, i * gw:(i + 1) * gw], parts[1][:, i * gw:(i + 1) * gw]], axis=1)
    s.q[:, cols] = (both(0) + s.bias_v[0:1, cols]).astype(bf16) * jnp.asarray(0.125, bf16)
    s.k[:, cols] = both(1).astype(bf16)
    s.v[:, cols] = (both(2) + s.bias_v[0:1, value_cols]).astype(bf16)


def stage_mask(s):
    T, D = s.x.shape
    place = lax.broadcasted_iota(jnp.int32, (1, T), 1)
    code = s.seg[...] * 1024 + (place - s.pos[...])
    keyed = jnp.where(s.tok[...] == 1, code, -1)
    keyed = jnp.broadcast_to(keyed.astype(f32), (128, T)).T
    code_f = code.astype(f32)
    for c in range(T // 128):
        cols = pl.ds(c * 128, 128)
        same = keyed == code_f[:, c * 128:(c + 1) * 128]
        rows = lax.broadcasted_iota(jnp.int32, (T, 128), 0)
        lanes = lax.broadcasted_iota(jnp.int32, (T, 128), 1) + c * 128
        s.mask[:, cols] = jnp.where(same | (rows == lanes), 0.0, -1000000000.0)


def stage_attn_fwd(s, lo, hi):
    T, D = s.x.shape
    lane = lax.broadcasted_iota(jnp.int32, (1, 128), 1)
    def pair_step(pr, carry):
        cols = pl.ds(pl.multiple_of(pr * 128, 128), 128)
        q2 = s.q[:, cols]
        k2 = s.k[:, cols]
        vT = s.v[:, cols].T
        outs = []
        for h in range(2):
            keep = (lane < 64) if h == 0 else (lane >= 64)
            qm = jnp.where(keep, q2, jnp.zeros_like(q2))
            sT = dot_nt(k2, qm) + s.mask[...]
            m = jnp.max(sT, axis=0, keepdims=True)
            e = jnp.exp(sT - m)
            l = jnp.sum(e, axis=0, keepdims=True)
            p = (e * (1.0 / l)).astype(bf16)
            s.pT[2 * pr + h] = p
            outs.append(dot(vT[64 * h:64 * h + 64], p))
        cT = jnp.concatenate(outs, axis=0).astype(bf16)
        s.ctxT[pl.ds(pl.multiple_of(pr * 128, 128), 128), :] = cT
        s.ctx[:, cols] = cT.T
        return carry
    lax.fori_loop(lo, hi, pair_step, 0)


def stage_ln1(s):
    T, D = s.x.shape
    s.att[...] = dot(s.ctx[...], s.wout[...])
    R = 32
    def step(i, carry):
        rows = pl.ds(pl.multiple_of(i * R, R), R)
        u = s.x[rows, :].astype(f32) + (s.att[rows, :] + s.bias(2 * D, 0, D))
        c = u - jnp.sum(u, axis=1, keepdims=True) * (1.0 / D)
        r = lax.rsqrt(jnp.sum(c * c, axis=1, keepdims=True) * (1.0 / D) + epsilon)
        n = c * r
        s.n1[rows, :] = n
        s.r1[rows, :] = jnp.broadcast_to(r, (R, 128))
        s.first_low[rows, :] = (n * s.gain(0) + s.bias(3 * D, 0, D)).astype(bf16)
        return carry
    lax.fori_loop(0, T // R, step, 0)


def gelu_parts(z):
    phi = 0.5 * (1.0 + lax.erf(z * 0.7071067811865476))
    dens = jnp.exp(z * z * -0.5) * 0.3989422804014327
    return z * phi, phi + z * dens


def stage_ffn(s):
    T, D = s.x.shape
    gw, fg = D // GROUPS, FF // GROUPS
    R = 128
    def step(i, carry):
        rows = pl.ds(pl.multiple_of(i * R, R), R)
        for pair in range(2):
            outs = []
            for g in (2 * pair, 2 * pair + 1):
                z = dot(s.first_low[rows, g * gw:(g + 1) * gw], s.wup[g]) + s.bias(4 * D, g * fg, fg)
                act, gp = gelu_parts(z)
                act = act.astype(bf16)
                s.active[rows, g * fg:(g + 1) * fg] = act
                s.gp[rows, g * fg:(g + 1) * fg] = gp
                outs.append(dot(act, s.wdown[g]))
            s.att[rows, pair * 2 * gw:(pair + 1) * 2 * gw] = jnp.concatenate(outs, axis=1)
        return carry
    lax.fori_loop(0, T // R, step, 0)


def stage_ln2(s):
    T, D = s.x.shape
    R = 32
    for a in (s.acc_g2, s.acc_s2, s.acc_down):
        a[...] = jnp.zeros_like(a)
    def step(i, carry):
        rows = pl.ds(pl.multiple_of(i * R, R), R)
        first = s.n1[rows, :] * s.gain(0) + s.bias(3 * D, 0, D)
        u = first + (s.att[rows, :] + s.bias(4 * D + FF, 0, D))
        c = u - jnp.sum(u, axis=1, keepdims=True) * (1.0 / D)
        r = lax.rsqrt(jnp.sum(c * c, axis=1, keepdims=True) * (1.0 / D) + epsilon)
        n = c * r
        s.out[rows, :] = (n * s.gain(D) + s.bias(5 * D + FF, 0, D)).astype(bf16)
        dy = s.cot[rows, :].astype(f32)
        s.acc_g2[...] += fold(dy * n)
        s.acc_s2[...] += fold(dy)
        e = dy * s.gain(D)
        m1 = jnp.sum(e, axis=1, keepdims=True) * (1.0 / D)
        m2 = jnp.sum(e * n, axis=1, keepdims=True) * (1.0 / D)
        du = r * (e - m1 - n * m2)
        s.dsec[rows, :] = du
        dl = du.astype(bf16)
        s.douter[rows, :] = dl
        s.acc_down[...] += fold(dl.astype(f32))
        return carry
    lax.fori_loop(0, T // R, step, 0)


def stage_ffn_back(s, lo, hi):
    T, D = s.x.shape
    gw, fg = D // GROUPS, FF // GROUPS
    R = 128
    if lo == 0:
        s.acc_up[...] = jnp.zeros_like(s.acc_up)
    def step(i, carry):
        rows = pl.ds(pl.multiple_of(i * R, R), R)
        for pair in range(2):
            outs = []
            for g in (2 * pair, 2 * pair + 1):
                da = dot_nt(s.douter[rows, g * gw:(g + 1) * gw], s.wdown[g])
                di = (da * s.gp[rows, g * fg:(g + 1) * fg]).astype(bf16)
                s.dinner[rows, g * fg:(g + 1) * fg] = di
                s.acc_up[:, g * fg:(g + 1) * fg] += fold(di.astype(f32))
                outs.append(dot_nt(di, s.wup[g]))
            s.att[rows, pair * 2 * gw:(pair + 1) * 2 * gw] = jnp.concatenate(outs, axis=1)
        return carry
    lax.fori_loop(T // R * lo // 4, T // R * hi // 4, step, 0)


def stage_down_grad(s, put):
    T, D = s.x.shape
    gw, fg = D // GROUPS, FF // GROUPS
    for g in range(GROUPS):
        put(g, dot_tn(s.active[:, g * fg:(g + 1) * fg], s.douter[:, g * gw:(g + 1) * gw]))


def stage_up_grad(s, put):
    T, D = s.x.shape
    gw, fg = D // GROUPS, FF // GROUPS
    for g in range(GROUPS):
        put(g, dot_tn(s.first_low[:, g * gw:(g + 1) * gw], s.dinner[:, g * fg:(g + 1) * fg]))


def stage_ln1_back(s):
    T, D = s.x.shape
    R = 32
    for a in (s.acc_g1, s.acc_s1, s.acc_out):
        a[...] = jnp.zeros_like(a)
    def step(i, carry):
        rows = pl.ds(pl.multiple_of(i * R, R), R)
        dy = s.dsec[rows, :] + s.att[rows, :]
        n = s.n1[rows, :]
        s.acc_g1[...] += fold(dy * n)
        s.acc_s1[...] += fold(dy)
        e = dy * s.gain(0)
        m1 = jnp.sum(e, axis=1, keepdims=True) * (1.0 / D)
        m2 = jnp.sum(e * n, axis=1, keepdims=True) * (1.0 / D)
        du = s.r1[rows, 0:1] * (e - m1 - n * m2)
        s.dsec[rows, :] = du
        dl = du.astype(bf16)
        s.dattn[rows, :] = dl
        s.acc_out[...] += fold(dl.astype(f32))
        return carry
    lax.fori_loop(0, T // R, step, 0)


def stage_out_grad(s, put):
    put(dot(s.ctxT[...], s.dattn[...]))
    s.dctx[...] = dot_nt(s.dattn[...], s.wout[...]).astype(bf16)


def stage_attn_back(s, lo, hi):
    T, D = s.x.shape
    lane = lax.broadcasted_iota(jnp.int32, (1, 128), 1)
    def pair_step(pr, carry):
        start = pl.multiple_of(pr * 128, 128)
        cols = pl.ds(start, 128)
        q2 = s.q[:, cols]
        v2 = s.v[:, cols]
        dc2 = s.dctx[:, cols]
        kT = s.k[:, cols].T
        prod = (s.ctxT[cols, :].astype(f32)) * (dc2.T.astype(f32))
        dk, dv, dqT = [], [], []
        for h in range(2):
            keep = (lane < 64) if h == 0 else (lane >= 64)
            qm = jnp.where(keep, q2, jnp.zeros_like(q2))
            dcm = jnp.where(keep, dc2, jnp.zeros_like(dc2))
            p = s.pT[2 * pr + h]
            delta = jnp.sum(prod[64 * h:64 * h + 64], axis=0, keepdims=True)
            dp = dot_nt(v2, dcm)
            ds = (p.astype(f32) * (dp - delta)).astype(bf16)
            dv.append(dot(p, dcm))
            dk.append(dot(ds, qm))
            dqT.append(dot(kT[64 * h:64 * h + 64], ds))
        s.dv[:, cols] = (dv[0] + dv[1]).astype(bf16)
        s.dk[:, cols] = (dk[0] + dk[1]).astype(bf16)
        s.dq[:, cols] = (jnp.concatenate(dqT, axis=0) * 0.125).astype(bf16).T
        return carry
    lax.fori_loop(lo, hi, pair_step, 0)


def stage_qkv_grad(s, half, put):
    T, D = s.x.shape
    gw = D // GROUPS
    cols = pl.ds(pl.multiple_of(half * 2 * gw, 128), 2 * gw)
    xh, dq, dk, dv = s.x[:, cols], s.dq[:, cols], s.dk[:, cols], s.dv[:, cols]
    for i in range(2):
        c = slice(i * gw, (i + 1) * gw)
        joined = jnp.concatenate([dq[:, c], dk[:, c], dv[:, c]], axis=1)
        s.joined[2 * half + i] = joined
        put(2 * half + i, i, dot_tn(xh[:, c], joined))


def stage_input_grad(s):
    T, D = s.x.shape
    gw = D // GROUPS
    for pair in range(2):
        cols = slice(pair * 2 * gw, (pair + 1) * 2 * gw)
        outs = [dot_nt(s.joined[g], s.wqkv[g]) for g in (2 * pair, 2 * pair + 1)]
        s.din[:, cols] = s.dsec[:, cols] + jnp.concatenate(outs, axis=1)


MESH = pl.DeviceIdType.MESH
ARRAYS = ("small", "qkv", "out", "up", "down")
NEAR = ("small", "qkv")


class Names:
    pass


class Torus:
    def __init__(self, sizes):
        self.nx, gy = sizes
        self.nc = 2
        assert gy % self.nc == 0
        self.nz = 4 if (gy // self.nc) % 4 == 0 else 1
        self.ny = gy // self.nc // self.nz
        self.count = self.nx * gy
        self.square = self.nx == 2 and self.ny == 2
        self.flat = self.ny * self.nz

    def locate(self):
        gy = lax.axis_index("gy")
        self.x = lax.axis_index("gx")
        self.c = gy % self.nc
        self.y = gy // self.nc % self.ny
        self.z = gy // (self.nc * self.ny)

    def device(self, x, y, z, c):
        return (x, (z * self.ny + y) * self.nc + c)

    def sibling(self):
        return self.device(self.x, self.y, self.z, 1 - self.c)

    def place(self, x, y, z, c):
        return ((c * self.nx + x) * self.ny + y) * self.nz + z

    def place_in(self, x, gy):
        return self.place(x, gy // self.nc % self.ny, gy // (self.nc * self.ny), gy % self.nc)

    def place_of(self, index):
        gy_size = self.flat * self.nc
        return self.place_in(index // gy_size, index % gy_size)

    def shift(self, o):
        return (self.x + o[0]) % self.nx, (self.y + o[1]) % self.ny

    def turn(self, o):
        return (self.y + o[0]) % self.ny, (self.z + o[1]) % self.nz

    def plane_offsets(self):
        return [(i, j) for i in range(self.nx) for j in range(self.ny) if i or j]

    def flat_offsets(self):
        return [(i, j) for j in range(self.nz) for i in range(self.ny) if i or j]

    def peers(self):
        found = [self.device(self.x, y, z, self.c) for y, z in (self.turn(o) for o in self.flat_offsets())]
        for o in self.plane_offsets():
            if o[0] == 0 or (self.square and o == (1, 1)):
                continue
            px, py = self.shift(o)
            found.append(self.device(px, py, self.z, self.c))
        return found + [self.sibling()]


def remote(src, dst, send, recv, device):
    return pltpu.make_async_remote_copy(
        src_ref=src, dst_ref=dst, send_sem=send, recv_sem=recv, device_id=device, device_id_type=MESH
    )


class NearGather:
    def __init__(self, t, own, buf, sems):
        self.t, self.own, self.buf = t, own, buf
        self.local, self.s1, self.r1, self.s2, self.r2, self.s3, self.r3 = sems

    def chunk(self, x, c):
        return self.buf.at[pl.ds(self.t.place(x, 0, 0, c), self.t.flat)]

    def local_copy(self):
        t = self.t
        return pltpu.make_async_copy(self.own, self.buf.at[t.place(t.x, t.y, t.z, t.c)], self.local.at[0])

    def near_copies(self):
        t = self.t
        mine = self.buf.at[t.place(t.x, t.y, t.z, t.c)]
        found = []
        for k, o in enumerate(t.flat_offsets()):
            py, pz = t.turn(o)
            found.append(remote(self.own, mine, self.s1.at[k], self.r1.at[k], t.device(t.x, py, pz, t.c)))
        return found

    def far_copy(self, d):
        t = self.t
        part = self.chunk(t.x, t.c)
        return remote(part, part, self.s2.at[d], self.r2.at[d], t.device((t.x + d) % t.nx, t.y, t.z, t.c))

    def core_copy(self, d):
        t = self.t
        part = self.chunk((t.x + t.nx - d) % t.nx, t.c)
        return remote(part, part, self.s3.at[d], self.r3.at[d], t.sibling())

    def begin(self):
        self.local_copy().start()
        for c in self.near_copies():
            c.start()

    def spread(self):
        for c in self.near_copies():
            c.wait_recv()
        self.local_copy().wait()
        self.core_copy(0).start()
        for d in range(1, self.t.nx):
            self.far_copy(d).start()

    def near_done(self):
        self.core_copy(0).wait_recv()

    def share(self):
        for d in range(1, self.t.nx):
            self.far_copy(d).wait_recv()
            self.core_copy(d).start()

    def far_done(self):
        for d in range(1, self.t.nx):
            self.core_copy(d).wait_recv()

    def close(self):
        for c in self.near_copies():
            c.wait_send()
        for d in range(self.t.nx):
            self.core_copy(d).wait_send()
            if d:
                self.far_copy(d).wait_send()


class NearScatter:
    def __init__(self, t, buf, ra, rb, rc, sems):
        self.t, self.buf, self.ra, self.rb, self.rc = t, buf, ra, rb, rc
        self.s1, self.r1, self.s2, self.r2, self.s3, self.r3 = sems

    def core_copy(self, d):
        t = self.t
        part = self.buf.at[pl.ds(t.place((t.x + d) % t.nx, 0, 0, 1 - t.c), t.flat)]
        return remote(part, self.ra.at[d], self.s1.at[d], self.r1.at[d], t.sibling())

    def far_copy(self, d):
        t = self.t
        return remote(self.ra.at[d], self.rb.at[d], self.s2.at[d], self.r2.at[d],
                      t.device((t.x + d) % t.nx, t.y, t.z, t.c))

    def flat_copy(self, k, o):
        t = self.t
        py, pz = t.turn(o)
        return remote(self.ra.at[0, py * t.nz + pz], self.rc.at[k], self.s3.at[k], self.r3.at[k],
                      t.device(t.x, py, pz, t.c))

    def chip_sum(self, d):
        t = self.t
        self.core_copy(d).wait_recv()
        part = self.buf[pl.ds(t.place((t.x + d) % t.nx, 0, 0, t.c), t.flat)]
        return part.astype(f32) + self.ra[d].astype(f32)

    def begin_far(self):
        for d in range(1, self.t.nx):
            self.core_copy(d).start()

    def far(self):
        for d in range(1, self.t.nx):
            self.ra[d] = self.chip_sum(d).astype(self.ra.dtype)
            self.far_copy(d).start()

    def begin_near(self):
        self.core_copy(0).start()

    def near(self):
        total = self.chip_sum(0)
        for d in range(1, self.t.nx):
            self.far_copy(d).wait_recv()
            total = total + self.rb[d].astype(f32)
        self.ra[0] = total.astype(self.ra.dtype)
        for k, o in enumerate(self.t.flat_offsets()):
            self.flat_copy(k, o).start()

    def total(self):
        t = self.t
        total = self.ra[0, t.y * t.nz + t.z].astype(f32)
        for k, o in enumerate(t.flat_offsets()):
            self.flat_copy(k, o).wait_recv()
            total = total + self.rc[k].astype(f32)
        return total

    def close(self):
        for k, o in enumerate(self.t.flat_offsets()):
            self.flat_copy(k, o).wait_send()
        for d in range(self.t.nx):
            self.core_copy(d).wait_send()
            if d:
                self.far_copy(d).wait_send()


class Planes:
    def route(self):
        t = self.t
        if t.square:
            self.offsets = [(t.c, 1 - t.c), (1 - t.c, t.c)]
        else:
            self.offsets = t.plane_offsets()

    def slot(self, o):
        return o[0] * self.t.ny + o[1]

    def to(self, o):
        px, py = self.t.shift(o)
        return self.t.device(px, py, self.t.z, self.t.c)


class Gather(Planes):
    def __init__(self, t, own, buf, sems):
        self.t, self.own, self.buf = t, own, buf
        self.local, self.s1, self.r1, self.s2, self.r2, self.s3, self.r3 = sems
        self.route()

    def chunk(self, x, y):
        return self.buf.at[pl.ds(self.t.place(x, y, 0, self.t.c), self.t.nz)]

    def local_copy(self):
        t = self.t
        return pltpu.make_async_copy(self.own, self.buf.at[t.place(t.x, t.y, t.z, t.c)], self.local.at[0])

    def line_copies(self):
        t = self.t
        mine = self.buf.at[t.place(t.x, t.y, t.z, t.c)]
        return [
            remote(self.own, mine, self.s1.at[d], self.r1.at[d], t.device(t.x, t.y, (t.z + d) % t.nz, t.c))
            for d in range(1, t.nz)
        ]

    def plane_copy(self, k):
        part = self.chunk(self.t.x, self.t.y)
        return remote(part, part, self.s2.at[k], self.r2.at[k], self.to(self.offsets[k]))

    def relay_copy(self):
        part = self.chunk(*self.t.shift(self.offsets[0]))
        return remote(part, part, self.s2.at[2], self.r2.at[2], self.to(self.offsets[1]))

    def core_copy(self, o):
        t = self.t
        part = self.chunk((t.x + t.nx - o[0]) % t.nx, (t.y + t.ny - o[1]) % t.ny)
        k = self.slot(o)
        return remote(part, part, self.s3.at[k], self.r3.at[k], t.sibling())

    def begin(self):
        self.local_copy().start()
        for c in self.line_copies():
            c.start()

    def spread(self):
        for c in self.line_copies():
            c.wait_recv()
        self.local_copy().wait()
        for k in range(len(self.offsets)):
            self.plane_copy(k).start()
        self.core_copy((0, 0)).start()

    def share(self):
        for k, o in enumerate(self.offsets):
            self.plane_copy(k).wait_recv()
            if self.t.square and k == 0:
                self.relay_copy().start()
            self.core_copy(o).start()

    def share_last(self):
        if self.t.square:
            self.relay_copy().wait_recv()
            self.core_copy((1, 1)).start()

    def done(self):
        for o in [(0, 0)] + self.t.plane_offsets():
            self.core_copy(o).wait_recv()

    def close(self):
        for c in self.line_copies():
            c.wait_send()
        for k in range(len(self.offsets)):
            self.plane_copy(k).wait_send()
        if self.t.square:
            self.relay_copy().wait_send()
        for o in [(0, 0)] + self.t.plane_offsets():
            self.core_copy(o).wait_send()


class Scatter(Planes):
    def __init__(self, t, buf, ra, rb, rc, sems):
        self.t, self.buf, self.ra, self.rb, self.rc = t, buf, ra, rb, rc
        self.s1, self.r1, self.s2, self.r2, self.s3, self.r3 = sems
        self.route()

    def core_copy(self, o):
        t = self.t
        px, py = t.shift(o)
        part = self.buf.at[pl.ds(t.place(px, py, 0, 1 - t.c), t.nz)]
        k = self.slot(o)
        return remote(part, self.ra.at[k], self.s1.at[k], self.r1.at[k], t.sibling())

    def plane_copy(self, k, o, to):
        return remote(self.ra.at[self.slot(o)], self.rb.at[k], self.s2.at[k], self.r2.at[k], self.to(to))

    def line_copy(self, d):
        t = self.t
        to = (t.z + d) % t.nz
        return remote(self.ra.at[0, to], self.rc.at[d], self.s3.at[d], self.r3.at[d], t.device(t.x, t.y, to, t.c))

    def hops(self):
        if self.t.square:
            a, b = self.offsets
            return [(0, (1, 1), b), (1, b, b), (2, a, a)]
        return [(k, o, o) for k, o in enumerate(self.offsets)]

    def chip_sum(self, o):
        t = self.t
        px, py = t.shift(o)
        part = self.buf[pl.ds(t.place(px, py, 0, t.c), t.nz)]
        return part.astype(f32) + self.ra[self.slot(o)].astype(f32)

    def begin(self):
        for o in self.t.plane_offsets() + [(0, 0)]:
            self.core_copy(o).start()

    def planes(self):
        for o in self.t.plane_offsets() + [(0, 0)]:
            self.core_copy(o).wait_recv()
        for k, o, to in self.hops()[:2] if self.t.square else self.hops():
            self.ra[self.slot(o)] = self.chip_sum(o).astype(self.ra.dtype)
            self.plane_copy(k, o, to).start()

    def planes_last(self):
        if self.t.square:
            hops = self.hops()
            self.plane_copy(*hops[0]).wait_recv()
            k, o, to = hops[2]
            self.ra[self.slot(o)] = (self.chip_sum(o) + self.rb[0].astype(f32)).astype(self.ra.dtype)
            self.plane_copy(k, o, to).start()

    def line(self):
        t = self.t
        total = self.chip_sum((0, 0))
        for k, o, to in self.hops()[1:] if t.square else self.hops():
            self.plane_copy(k, o, to).wait_recv()
            total = total + self.rb[k].astype(f32)
        self.ra[0] = total.astype(self.ra.dtype)
        for d in range(1, t.nz):
            self.line_copy(d).start()

    def total(self):
        t = self.t
        total = self.ra[0, t.z].astype(f32)
        for d in range(1, t.nz):
            self.line_copy(d).wait_recv()
            total = total + self.rc[d].astype(f32)
        return total

    def close(self):
        for d in range(1, self.t.nz):
            self.line_copy(d).wait_send()
        for hop in self.hops():
            self.plane_copy(*hop).wait_send()
        for o in self.t.plane_offsets() + [(0, 0)]:
            self.core_copy(o).wait_send()


def swap_halves(a, b):
    lane = lax.broadcasted_iota(jnp.int32, a.shape, 1)
    return jnp.where(lane < 64, pltpu.roll(a, 64, 1), pltpu.roll(b, 64, 1))


def lines_to_rows(lines, spare, rows, width):
    if width % 128 == 0:
        m = width // 128
        return jnp.concatenate([lines[pl.ds(j, rows, stride=m), :] for j in range(m)], axis=1).astype(bf16)
    m = width // 64
    q, half = m // 2, rows // 2
    a = [lines[pl.ds(j, half, stride=m), :] for j in range(m)]
    for j in range(q + 1):
        spare[j, pl.ds(0, half, stride=2), :] = a[j]
        spare[j, pl.ds(1, half, stride=2), :] = swap_halves(a[q + j], a[q + j + 1] if j < q else a[q + j])
    return jnp.concatenate([spare[j] for j in range(q)] + [spare[q][:, 0:64]], axis=1).astype(bf16)


def rows_to_lines(value, lines, spare):
    rows, width = value.shape
    if width % 128 == 0:
        m = width // 128
        for j in range(m):
            lines[pl.ds(j, rows, stride=m), :] = value[:, 128 * j:128 * j + 128]
        return
    m = width // 64
    q, half = m // 2, rows // 2
    for j in range(q):
        spare[j] = value[:, 128 * j:128 * j + 128]
    spare[q, :, 0:64] = value[:, 128 * q:width]
    even = [spare[j, pl.ds(0, half, stride=2), :] for j in range(q + 1)]
    odd = [spare[j, pl.ds(1, half, stride=2), :] for j in range(q + 1)]
    lane = lax.broadcasted_iota(jnp.int32, even[0].shape, 1)
    for j in range(q):
        lines[pl.ds(j, half, stride=m), :] = even[j]
        lines[pl.ds(q + 1 + j, half, stride=m), :] = swap_halves(odd[j], odd[j + 1])
    lines[pl.ds(q, half, stride=m), :] = jnp.where(lane < 64, even[q], pltpu.roll(odd[0], 64, 1))


def group_places(t, g, half, i):
    per = t.count // GROUPS
    if t.nx == 2:
        return [t.place_in(half, i * per + j) for j in range(per)]
    return [t.place_of(g * per + j) for j in range(per)]


def group_weight(s, t, name, places):
    buf = s.held[name]
    rows, width = s.group_shape[name]
    if s.lined:
        n = buf.shape[1]
        for j, p in enumerate(places):
            s.lines[n * j:n * j + n, :] = buf[p].astype(f32)
        return lines_to_rows(s.lines, s.spare[width], rows, width)
    return jnp.concatenate([buf[p].astype(f32) for p in places], axis=0).astype(bf16)


def assemble_small(s, t):
    nb, ng = s.small_sizes
    buf = s.held["small"]
    for d in range(t.count):
        p = t.place_of(d)
        s.bias_v[0:1, nb * d:nb * d + nb] = buf[p, 0:1, 0:nb]
        s.gain_v[0:1, ng * d:ng * d + ng] = buf[p, 0:1, nb:nb + ng]


def assemble_qkv(s, t, half):
    for i in range(2):
        g = 2 * half + i
        s.wqkv[g] = group_weight(s, t, "qkv", group_places(t, g, half, i))


def assemble(s, t, name):
    for g in range(GROUPS):
        value = group_weight(s, t, name, group_places(t, g, g // 2, g % 2))
        if name == "out":
            gw = s.wout.shape[0] // GROUPS
            s.wout[g * gw:(g + 1) * gw, :] = value
        elif name == "up":
            s.wup[g] = value
        else:
            s.wdown[g] = value


def lay_out(s, t, name, places, value):
    buf = s.held[name]
    if s.lined:
        n = buf.shape[1]
        rows_to_lines(value, s.lines, s.spare[value.shape[1]] if value.shape[1] % 128 else None)
        for j, p in enumerate(places):
            buf[p] = s.lines[n * j:n * j + n, :].astype(bf16)
        return
    rows = value.shape[0] // len(places)
    for j, p in enumerate(places):
        buf[p] = value[rows * j:rows * j + rows].astype(bf16)


def lay_out_small(s, t):
    T, D = s.x.shape
    nb, ng = s.small_sizes
    def rs(v):
        return jnp.sum(v, axis=0, keepdims=True)
    s.bias_v[:, 0:D] = rs(s.dq[...].astype(f32))
    s.bias_v[:, D:2 * D] = rs(s.dv[...].astype(f32))
    s.bias_v[:, 2 * D:3 * D] = rs(s.acc_out[...])
    s.bias_v[:, 3 * D:4 * D] = rs(s.acc_s1[...])
    s.bias_v[:, 4 * D:4 * D + FF] = rs(s.acc_up[...])
    s.bias_v[:, 4 * D + FF:5 * D + FF] = rs(s.acc_down[...])
    s.bias_v[:, 5 * D + FF:] = rs(s.acc_s2[...])
    s.gain_v[:, 0:D] = rs(s.acc_g1[...])
    s.gain_v[:, D:] = rs(s.acc_g2[...])
    buf = s.held["small"]
    for d in range(t.count):
        p = t.place_of(d)
        buf[p, 0:1, 0:nb] = s.bias_v[0:1, nb * d:nb * d + nb]
        buf[p, 0:1, nb:nb + ng] = s.gain_v[0:1, ng * d:ng * d + ng]


def layer_kernel(names, t, small_sizes, group_shape, lined, *refs):
    s = Names()
    for n, r in zip(names, refs, strict=True):
        setattr(s, n, r)
    D = s.x.shape[1]
    nb, ng = small_sizes
    s.small_sizes, s.group_shape, s.lined = small_sizes, group_shape, lined
    s.bias = lambda base, off, w: s.bias_v[0:1, base + off:base + off + w]
    s.gain = lambda base: s.gain_v[0:1, base:base + D]
    s.held = {n: getattr(s, "held_" + n) for n in ARRAYS}
    if lined:
        s.spare = {D // GROUPS * 3: s.spare_wide, D // GROUPS: s.spare_tall, D: None}
    t.locate()

    barrier = pltpu.get_barrier_semaphore()
    peers = t.peers()
    for peer in peers:
        pl.semaphore_signal(barrier, inc=1, device_id=peer, device_id_type=MESH)
    pl.semaphore_wait(barrier, len(peers))

    gather, scatter = {}, {}
    for i, n in enumerate(ARRAYS):
        make = (NearGather, NearScatter) if n in NEAR else (Gather, Scatter)
        gather[n] = make[0](t, getattr(s, "in_" + n), s.held[n],
                            [getattr(s, "g_" + k).at[i] for k in ("local", "s1", "r1", "s2", "r2", "s3", "r3")])
        scatter[n] = make[1](t, s.held[n], *[getattr(s, k + "_" + n) for k in ("ra", "rb", "rc")],
                             [getattr(s, "h_" + k).at[i] for k in ("s1", "r1", "s2", "r2", "s3", "r3")])
    near_first = t.nx == 2
    half = t.x if near_first else 0
    rest = 1 - half

    take_x = pltpu.make_async_copy(s.x_in, s.x, s.moves.at[0])
    take_cot = pltpu.make_async_copy(s.cot_in, s.cot, s.moves.at[1])
    give_out = pltpu.make_async_copy(s.out, s.out_to, s.moves.at[2])
    give_din = pltpu.make_async_copy(s.din, s.din_to, s.moves.at[3])

    gather["small"].begin()
    gather["qkv"].begin()
    take_x.start()
    take_cot.start()
    stage_mask(s)
    gather["small"].spread()
    gather["small"].share()
    gather["qkv"].spread()
    gather["out"].begin()
    gather["up"].begin()
    gather["down"].begin()
    gather["small"].near_done()
    gather["small"].far_done()
    assemble_small(s, t)
    take_x.wait()
    gather["qkv"].near_done()
    if not near_first:
        gather["qkv"].share()
        gather["qkv"].far_done()
    assemble_qkv(s, t, half)
    stage_qkv(s, half)
    stage_attn_fwd(s, 3 * half, 3 * half + 1)
    gather["out"].spread()
    stage_attn_fwd(s, 3 * half + 1, 3 * half + 2)
    if near_first:
        gather["qkv"].share()
    gather["up"].spread()
    stage_attn_fwd(s, 3 * half + 2, 3 * half + 3)
    gather["down"].spread()
    if near_first:
        gather["qkv"].far_done()
    assemble_qkv(s, t, rest)
    stage_qkv(s, rest)
    stage_attn_fwd(s, 3 * rest, 3 * rest + 1)
    gather["out"].share()
    stage_attn_fwd(s, 3 * rest + 1, 3 * rest + 2)
    gather["out"].share_last()
    gather["up"].share()
    stage_attn_fwd(s, 3 * rest + 2, 3 * rest + 3)
    gather["down"].share()
    gather["out"].done()
    assemble(s, t, "out")
    gather["up"].share_last()
    stage_ln1(s)
    gather["down"].share_last()
    gather["up"].done()
    assemble(s, t, "up")
    gather["down"].done()
    assemble(s, t, "down")
    for n in ARRAYS:
        gather[n].close()
    stage_ffn(s)
    take_cot.wait()
    stage_ln2(s)
    give_out.start()

    def put(name):
        return lambda g, v: lay_out(s, t, name, group_places(t, g, g // 2, g % 2), v)

    stage_down_grad(s, put("down"))
    scatter["down"].begin()
    stage_ffn_back(s, 0, 2)
    scatter["down"].planes()
    stage_ffn_back(s, 2, 4)
    stage_up_grad(s, put("up"))
    scatter["up"].begin()
    stage_ln1_back(s)
    scatter["up"].planes()
    def put_out(v):
        gw = D // GROUPS
        for g in range(GROUPS):
            put("out")(g, v[g * gw:(g + 1) * gw])
    stage_out_grad(s, put_out)
    scatter["out"].begin()
    scatter["down"].planes_last()
    stage_attn_back(s, 3 * rest, 3 * rest + 1)
    scatter["out"].planes()
    stage_attn_back(s, 3 * rest + 1, 3 * rest + 2)
    scatter["up"].planes_last()
    stage_attn_back(s, 3 * rest + 2, 3 * rest + 3)
    scatter["down"].line()
    put_qkv = lambda h: lambda g, i, v: lay_out(s, t, "qkv", group_places(t, g, h, i), v)
    stage_qkv_grad(s, rest, put_qkv(rest))
    if near_first:
        scatter["qkv"].begin_far()
    stage_attn_back(s, 3 * half, 3 * half + 1)
    if near_first:
        scatter["qkv"].far()
    scatter["out"].planes_last()
    stage_attn_back(s, 3 * half + 1, 3 * half + 2)
    scatter["up"].line()
    s.grad_down[...] = scatter["down"].total()
    stage_attn_back(s, 3 * half + 2, 3 * half + 3)
    scatter["out"].line()
    stage_qkv_grad(s, half, put_qkv(half))
    if not near_first:
        scatter["qkv"].begin_far()
        scatter["qkv"].far()
    scatter["qkv"].begin_near()
    lay_out_small(s, t)
    scatter["small"].begin_far()
    scatter["small"].begin_near()
    scatter["qkv"].near()
    scatter["small"].far()
    stage_input_grad(s)
    give_din.start()
    scatter["small"].near()
    s.grad_up[...] = scatter["up"].total()
    s.grad_out[...] = scatter["out"].total()
    s.grad_qkv[...] = scatter["qkv"].total()
    small = scatter["small"].total()
    s.grad_bias[...] = small[:, 0:nb]
    s.grad_gain[...] = small[:, nb:nb + ng]
    give_out.wait()
    give_din.wait()
    for n in ARRAYS:
        scatter[n].close()


def hand_on(count, *refs):
    held, sems = refs[2 * count:3 * count], refs[3 * count]
    taken = [pltpu.make_async_copy(refs[i], held[i], sems.at[0, i]) for i in range(count)]
    given = [pltpu.make_async_copy(held[i], refs[count + i], sems.at[1, i]) for i in range(count)]
    for c in taken:
        c.start()
    for i in range(count):
        taken[i].wait()
        given[i].start()
    for c in given:
        c.wait()


def body(sizes, hidden_in, segment_ids, positions, token_mask, cotangent, qkv_weight, out_weight, up_weight, down_weight, biases, gains):
    rows, T, D = hidden_in.shape
    assert rows == 1
    gw, fg = D // GROUPS, FF // GROUPS
    t = Torus(sizes)
    nb, ng = biases.shape[0], gains.shape[0]
    depth = D // t.count
    group_shape = {"qkv": (gw, 3 * gw), "out": (gw, D), "up": (gw, fg), "down": (fg, gw)}
    lined = all(v.shape[0] % 512 == 0 for v in (qkv_weight, out_weight, up_weight, down_weight))
    blocks = {"small": ((1, nb + ng), f32)}
    for n, flat in zip(ARRAYS[1:], (qkv_weight, out_weight, up_weight, down_weight)):
        size = flat.shape[0]
        blocks[n] = ((size // 128, 128) if lined else (size // group_shape[n][1], group_shape[n][1]), bf16)
    inputs = {
        "x_in": hidden_in[0], "seg": segment_ids, "pos": positions, "tok": token_mask, "cot_in": cotangent[0],
        "in_small": jnp.concatenate([biases, gains]).astype(f32).reshape(1, nb + ng),
        "in_qkv": qkv_weight.reshape(blocks["qkv"][0]),
        "in_out": out_weight.reshape(blocks["out"][0]),
        "in_up": up_weight.reshape(blocks["up"][0]),
        "in_down": down_weight.reshape(blocks["down"][0]),
    }
    outputs = {"out_to": ((T, D), bf16), "din_to": ((T, D), f32)}
    for n in ARRAYS[1:]:
        outputs["grad_" + n] = (blocks[n][0], f32)
    outputs["grad_bias"] = ((1, nb), f32)
    outputs["grad_gain"] = ((1, ng), f32)
    scratch = dict(
        x=((T, D), bf16), cot=((T, D), bf16), out=((T, D), bf16), din=((T, D), f32),
        mask=((T, T), f32), q=((T, D), bf16), k=((T, D), bf16), v=((T, D), bf16), pT=((HEADS, T, T), bf16),
        ctx=((T, D), bf16), ctxT=((D, T), bf16), att=((T, D), f32), n1=((T, D), f32), r1=((T, 128), f32),
        first_low=((T, D), bf16), active=((T, FF), bf16), gp=((T, FF), f32), dsec=((T, D), f32),
        douter=((T, D), bf16), dinner=((T, FF), bf16), dattn=((T, D), bf16), dctx=((T, D), bf16),
        dq=((T, D), bf16), dk=((T, D), bf16), dv=((T, D), bf16), joined=((GROUPS, T, 3 * gw), bf16),
        acc_g2=((8, D), f32), acc_s2=((8, D), f32), acc_down=((8, D), f32), acc_up=((8, FF), f32),
        acc_g1=((8, D), f32), acc_s1=((8, D), f32), acc_out=((8, D), f32),
        bias_v=((1, nb * t.count), f32), gain_v=((1, ng * t.count), f32),
        wqkv=((GROUPS, gw, 3 * gw), bf16), wout=((D, D), bf16), wup=((GROUPS, gw, fg), bf16),
        wdown=((GROUPS, fg, gw), bf16),
    )
    if lined:
        scratch["lines"] = ((fg * gw // 128, 128), f32)
        scratch["spare_wide"] = ((3 * gw // 128 + 1, gw, 128), f32)
        scratch["spare_tall"] = ((gw // 128 + 1, fg, 128), f32)
    planes = t.nx * t.ny
    for n in ARRAYS:
        shape, kind = blocks[n]
        scratch["held_" + n] = ((t.count,) + shape, kind)
        near = n in NEAR
        scratch["ra_" + n] = ((t.nx, t.flat) if near else (planes, t.nz)) + shape, kind
        scratch["rb_" + n] = ((t.nx, t.flat) if near else (planes - 1, t.nz)) + shape, kind
        scratch["rc_" + n] = ((t.flat - 1,) if near else (t.nz,)) + shape, kind
    shapes = [pltpu.VMEM(*scratch[n]) for n in scratch]
    most = max(planes, t.flat)
    sems = ["g_local", "g_s1", "g_r1", "g_s2", "g_r2", "g_s3", "g_r3", "h_s1", "h_r1", "h_s2", "h_r2", "h_s3", "h_r3"]
    shapes += [pltpu.SemaphoreType.DMA((len(ARRAYS), most)) for n in sems]
    shapes.append(pltpu.SemaphoreType.DMA((4,)))
    names = list(inputs) + list(outputs) + list(scratch) + list(sems) + ["moves"]
    vm = pl.BlockSpec(memory_space=pltpu.VMEM)
    anywhere = pl.BlockSpec(memory_space=pl.ANY)
    found = pl.pallas_call(
        lambda *refs: layer_kernel(names, t, (nb, ng), group_shape, lined, *refs),
        out_shape=[jax.ShapeDtypeStruct(*outputs[n]) for n in outputs],
        in_specs=[anywhere if n in ("x_in", "cot_in") else vm for n in inputs],
        out_specs=[anywhere if n in ("out_to", "din_to") else vm for n in outputs],
        scratch_shapes=shapes,
        compiler_params=pltpu.CompilerParams(
            collective_id=0, has_side_effects=True, vmem_limit_bytes=67043328
        ),
        name="layer",
    )(*inputs.values())
    count = len(outputs)
    found = pl.pallas_call(
        lambda *refs: hand_on(count, *refs),
        out_shape=[jax.ShapeDtypeStruct(*outputs[n]) for n in outputs],
        in_specs=[anywhere] * count,
        out_specs=[anywhere] * count,
        scratch_shapes=[pltpu.VMEM(*outputs[n]) for n in outputs] + [pltpu.SemaphoreType.DMA((2, count))],
        name="hand_on",
    )(*found)
    o = dict(zip(outputs, found))
    return (
        o["out_to"][None], o["din_to"][None], o["grad_qkv"].reshape(-1), o["grad_out"].reshape(-1), o["grad_up"].reshape(-1),
        o["grad_down"].reshape(-1), o["grad_bias"].reshape(-1), o["grad_gain"].reshape(-1),
    )


def solution(mesh):
    whole = P(("gx", "gy"))
    rows2 = P(("gx", "gy"), None)
    rows3 = P(("gx", "gy"), None, None)
    sizes = (mesh.shape["gx"], mesh.shape["gy"])
    return jax.shard_map(
        lambda *args: body(sizes, *args),
        mesh=mesh,
        in_specs=(rows3, rows2, rows2, rows2, rows3) + (whole,) * 6,
        out_specs=(rows3, rows3) + (whole,) * 6,
        check_vma=False,
    )
```

time: 124 us -> 102 us (0.82)
  local copies, waits for them, and re-layouts: 17.9 us -> 0.66 us
  Pallas kernels: 103 us -> 99 us
    reshape x8 -> x0, local copies, waits for them, and re-layouts: 12 us -> none  [the longest x1 1.62 us: body(): o['grad_down'].reshape(-1)]
    pallas_call x1 -> x2, Pallas kernels: 103 us -> 99 us  [the longest x1 96 us: body(): pl.pallas_call(lambda *refs: layer_kernel(names, t, (nb, ng), group_shape...]
    unnamed x4 -> x0, local copies, waits for them, and re-layouts: 3.21 us -> none
    slice x1 -> x0, local copies, waits for them, and re-layouts: 1.38 us -> none  [body(): o['grad_small'][0, :nb]]
    broadcast_in_dim x2 -> x0, other arithmetic: 1.31 us -> none  [the longest x1 0.66 us: body(): jnp.pad(biases.astype(f32), (0, 256 - nb))[None]]
    convert_element_type x0 -> x1, other arithmetic: none -> 1.29 us  [body(): jnp.concatenate([biases, gains]).astype(f32).reshape(1, nb + ng)]
where the time goes in v2:
time: 102 us
  Pallas kernels  99 us (97%)
  other arithmetic  1.29 us (1%)
    pallas_call x1, Pallas kernels, body(): pl.pallas_call(lambda *refs: layer_kernel(names, t, (nb, ng), group_shape...  96 us
    pallas_call x1, Pallas kernels, body(): pl.pallas_call(lambda *refs: hand_on(count, *refs), out_shape=[jax.ShapeD...  3.02 us

profile of v2, /device:TPU:0, one launch (start us, length us, event | category | flops | bytes accessed | tf_op | source)
XLA Modules:
  0.0 101.8 jit_solution(8367767493813043151)
XLA Ops:
  0.6 0.7 concatenate.14
  1.3 1.3 %maximum_convert_fusion.refs_5_ = f32[1,288]{1,0:T(1,128)} fusion(bf16[1,48]{1,0:T(2,128)(2,1)} %bitcast.21, bf16[1,240]{1,0:T(2,128)(2,1)S(1)} %concatenate.14), kind=kLoop, calls=%fused_computation | loop fusion | flops 1152 | bytes 1728 | tf_op jit(solution)/shard_map/convert_element_type | solution.py:941
  2.6 96.0 %layer.1 = (bf16[512,768]{1,0:T(8,128)(2,1)}, f32[512,768]{1,0:T(8,128)}, f32[108,128]{1,0:T(8,128)}, f32[144,128]{1,0:T(8,128)}, f32[144,128]{1,0:T(8,128)}, /*...) custom-call(bf16[512,768]{1,0:T(8,128)(2,1)} %bitcast.15, s32[1,512]{1,0:T(1,128)} %refs_1_.1, ...), custom_call_target="tpu_custom_call" | custom-call | tf_op jit(solution)/shard_map/layer/pallas_call | solution.py:985
  98.6 3.0 %hand_on.1 = (bf16[512,768]{1,0:T(8,128)(2,1)}, f32[512,768]{1,0:T(8,128)}, f32[108,128]{1,0:T(8,128)}, f32[144,128]{1,0:T(8,128)}, f32[144,128]{1,0:T(8,128)}, ...) custom-call(bf16[512,768]{1,0:T(8,128)(2,1)} %get-tuple-element.24.refs_0_, ...), custom_call_target="tpu_custom_call" | custom-call | tf_op jit(solution)/shard_map/hand_on/pallas_call | solution.py:997

commit v3 on v2

--- a/solution.py
+++ b/solution.py
@@ -257,6 +257,16 @@
         put(2 * half + i, i, dot_tn(xh[:, c], joined))
 
 
+def stage_qkv_grad_one(s, half, i, put):
+    T, D = s.x.shape
+    gw = D // GROUPS
+    cols = pl.ds(pl.multiple_of(half * 2 * gw, 128), 2 * gw)
+    xh, dq, dk, dv = (lax.select_n(i == 0, v[:, gw:], v[:, :gw]) for v in (s.x[:, cols], s.dq[:, cols], s.dk[:, cols], s.dv[:, cols]))
+    joined = jnp.concatenate([dq, dk, dv], axis=1)
+    s.joined[2 * half + i] = joined
+    put(2 * half + i, i, dot_tn(xh, joined))
+
+
 def stage_input_grad(s):
     T, D = s.x.shape
     gw = D // GROUPS
@@ -285,6 +295,8 @@
         self.count = self.nx * gy
         self.square = self.nx == 2 and self.ny == 2
         self.flat = self.ny * self.nz
+        self.near_first = self.nx == 2
+        self.quads = self.near_first and self.nz == 4
 
     def locate(self):
         gy = lax.axis_index("gy")
@@ -302,12 +314,16 @@
     def place(self, x, y, z, c):
         return ((c * self.nx + x) * self.ny + y) * self.nz + z
 
-    def place_in(self, x, gy):
-        return self.place(x, gy // self.nc % self.ny, gy // (self.nc * self.ny), gy % self.nc)
-
-    def place_of(self, index):
+    def near_place(self, x, y, z, c):
+        return ((c * self.nx + x) * self.nz + z) * self.ny + y
+
+    def place_in(self, x, gy, near):
+        place = self.near_place if near else self.place
+        return place(x, gy // self.nc % self.ny, gy // (self.nc * self.ny), gy % self.nc)
+
+    def place_of(self, index, near):
         gy_size = self.flat * self.nc
-        return self.place_in(index // gy_size, index % gy_size)
+        return self.place_in(index // gy_size, index % gy_size, near)
 
     def shift(self, o):
         return (self.x + o[0]) % self.nx, (self.y + o[1]) % self.ny
@@ -343,15 +359,15 @@
         self.local, self.s1, self.r1, self.s2, self.r2, self.s3, self.r3 = sems
 
     def chunk(self, x, c):
-        return self.buf.at[pl.ds(self.t.place(x, 0, 0, c), self.t.flat)]
+        return self.buf.at[pl.ds(self.t.near_place(x, 0, 0, c), self.t.flat)]
 
     def local_copy(self):
         t = self.t
-        return pltpu.make_async_copy(self.own, self.buf.at[t.place(t.x, t.y, t.z, t.c)], self.local.at[0])
+        return pltpu.make_async_copy(self.own, self.buf.at[t.near_place(t.x, t.y, t.z, t.c)], self.local.at[0])
 
     def near_copies(self):
         t = self.t
-        mine = self.buf.at[t.place(t.x, t.y, t.z, t.c)]
+        mine = self.buf.at[t.near_place(t.x, t.y, t.z, t.c)]
         found = []
         for k, o in enumerate(t.flat_offsets()):
             py, pz = t.turn(o)
@@ -407,9 +423,22 @@
         self.t, self.buf, self.ra, self.rb, self.rc = t, buf, ra, rb, rc
         self.s1, self.r1, self.s2, self.r2, self.s3, self.r3 = sems
 
-    def core_copy(self, d):
-        t = self.t
-        part = self.buf.at[pl.ds(t.place((t.x + d) % t.nx, 0, 0, 1 - t.c), t.flat)]
+    halves = False
+
+    def turn(self, o):
+        t = self.t
+        if not self.halves:
+            return t.turn(o)
+        return (t.y + o[0]) % 2, (t.z // 2 + o[1]) % 2 * 2 + (t.z + o[2]) % 2
+
+    def offsets(self):
+        if not self.halves:
+            return [self.t.flat_offsets()]
+        return [[(i, a, b) for i in range(2) for b in range(2) if i or a or b] for a in range(2)]
+
+    def far_core_copy(self, d):
+        t = self.t
+        part = self.buf.at[pl.ds(t.near_place((t.x + d) % t.nx, 0, 0, 1 - t.c), t.flat)]
         return remote(part, self.ra.at[d], self.s1.at[d], self.r1.at[d], t.sibling())
 
     def far_copy(self, d):
@@ -417,54 +446,80 @@
         return remote(self.ra.at[d], self.rb.at[d], self.s2.at[d], self.r2.at[d],
                       t.device((t.x + d) % t.nx, t.y, t.z, t.c))
 
-    def flat_copy(self, k, o):
-        t = self.t
-        py, pz = t.turn(o)
-        return remote(self.ra.at[0, py * t.nz + pz], self.rc.at[k], self.s3.at[k], self.r3.at[k],
-                      t.device(t.x, py, pz, t.c))
-
-    def chip_sum(self, d):
-        t = self.t
-        self.core_copy(d).wait_recv()
-        part = self.buf[pl.ds(t.place((t.x + d) % t.nx, 0, 0, t.c), t.flat)]
-        return part.astype(f32) + self.ra[d].astype(f32)
+    def span(self, part):
+        t = self.t
+        if not self.halves:
+            return 0, t.flat
+        return (t.z // 2 + part) % 2 * 2 * t.ny, 2 * t.ny
+
+    def core_copy(self, part):
+        t = self.t
+        start, n = self.span(part)
+        k = part * t.nx
+        return remote(self.buf.at[pl.ds(t.near_place(t.x, 0, 0, 1 - t.c) + start, n)], self.ra.at[0, pl.ds(start, n)],
+                      self.s1.at[k], self.r1.at[k], t.sibling())
+
+    def flat_copies(self, part):
+        t = self.t
+        lists = self.offsets()
+        first = sum(len(l) for l in lists[:part])
+        found = []
+        for k, o in enumerate(lists[part]):
+            py, pz = self.turn(o)
+            found.append(remote(self.ra.at[0, pz * t.ny + py], self.rc.at[first + k], self.s3.at[first + k],
+                                self.r3.at[first + k], t.device(t.x, py, pz, t.c)))
+        return found
 
     def begin_far(self):
         for d in range(1, self.t.nx):
-            self.core_copy(d).start()
+            self.far_core_copy(d).start()
 
     def far(self):
-        for d in range(1, self.t.nx):
-            self.ra[d] = self.chip_sum(d).astype(self.ra.dtype)
+        t = self.t
+        for d in range(1, t.nx):
+            self.far_core_copy(d).wait_recv()
+            part = self.buf[pl.ds(t.near_place((t.x + d) % t.nx, 0, 0, t.c), t.flat)]
+            self.ra[d] = (part.astype(f32) + self.ra[d].astype(f32)).astype(self.ra.dtype)
             self.far_copy(d).start()
 
-    def begin_near(self):
-        self.core_copy(0).start()
-
-    def near(self):
-        total = self.chip_sum(0)
-        for d in range(1, self.t.nx):
-            self.far_copy(d).wait_recv()
-            total = total + self.rb[d].astype(f32)
-        self.ra[0] = total.astype(self.ra.dtype)
-        for k, o in enumerate(self.t.flat_offsets()):
-            self.flat_copy(k, o).start()
+    def begin_near(self, part):
+        self.core_copy(part).start()
+
+    def near(self, part):
+        t = self.t
+        start, n = self.span(part)
+        self.core_copy(part).wait_recv()
+        if part == len(self.offsets()) - 1:
+            for d in range(1, t.nx):
+                self.far_copy(d).wait_recv()
+        own = self.buf[pl.ds(t.near_place(t.x, 0, 0, t.c) + start, n)]
+        total = own.astype(f32) + self.ra[0, pl.ds(start, n)].astype(f32)
+        for d in range(1, t.nx):
+            total = total + self.rb[d, pl.ds(start, n)].astype(f32)
+        self.ra[0, pl.ds(start, n)] = total.astype(self.ra.dtype)
+        for c in self.flat_copies(part):
+            c.start()
 
     def total(self):
         t = self.t
-        total = self.ra[0, t.y * t.nz + t.z].astype(f32)
-        for k, o in enumerate(t.flat_offsets()):
-            self.flat_copy(k, o).wait_recv()
-            total = total + self.rc[k].astype(f32)
+        total = self.ra[0, t.z * t.ny + t.y].astype(f32)
+        k = 0
+        for part in range(len(self.offsets())):
+            for c in self.flat_copies(part):
+                c.wait_recv()
+                total = total + self.rc[k].astype(f32)
+                k += 1
         return total
 
     def close(self):
-        for k, o in enumerate(self.t.flat_offsets()):
-            self.flat_copy(k, o).wait_send()
-        for d in range(self.t.nx):
-            self.core_copy(d).wait_send()
-            if d:
-                self.far_copy(d).wait_send()
+        t = self.t
+        for part in range(len(self.offsets())):
+            self.core_copy(part).wait_send()
+            for c in self.flat_copies(part):
+                c.wait_send()
+        for d in range(1, t.nx):
+            self.far_core_copy(d).wait_send()
+            self.far_copy(d).wait_send()
 
 
 class Planes:
@@ -676,11 +731,11 @@
     lines[pl.ds(q, half, stride=m), :] = jnp.where(lane < 64, even[q], pltpu.roll(odd[0], 64, 1))
 
 
-def group_places(t, g, half, i):
+def group_places(t, g, half, i, near):
     per = t.count // GROUPS
     if t.nx == 2:
-        return [t.place_in(half, i * per + j) for j in range(per)]
-    return [t.place_of(g * per + j) for j in range(per)]
+        return [t.place_in(half, i * per + j, near) for j in range(per)]
+    return [t.place_of(g * per + j, near) for j in range(per)]
 
 
 def group_weight(s, t, name, places):
@@ -698,7 +753,7 @@
     nb, ng = s.small_sizes
     buf = s.held["small"]
     for d in range(t.count):
-        p = t.place_of(d)
+        p = t.place_of(d, True)
         s.bias_v[0:1, nb * d:nb * d + nb] = buf[p, 0:1, 0:nb]
         s.gain_v[0:1, ng * d:ng * d + ng] = buf[p, 0:1, nb:nb + ng]
 
@@ -706,12 +761,12 @@
 def assemble_qkv(s, t, half):
     for i in range(2):
         g = 2 * half + i
-        s.wqkv[g] = group_weight(s, t, "qkv", group_places(t, g, half, i))
+        s.wqkv[g] = group_weight(s, t, "qkv", group_places(t, g, half, i, True))
 
 
 def assemble(s, t, name):
     for g in range(GROUPS):
-        value = group_weight(s, t, name, group_places(t, g, g // 2, g % 2))
+        value = group_weight(s, t, name, group_places(t, g, g // 2, g % 2, False))
         if name == "out":
             gw = s.wout.shape[0] // GROUPS
             s.wout[g * gw:(g + 1) * gw, :] = value
@@ -750,7 +805,7 @@
     s.gain_v[:, D:] = rs(s.acc_g2[...])
     buf = s.held["small"]
     for d in range(t.count):
-        p = t.place_of(d)
+        p = t.place_of(d, True)
         buf[p, 0:1, 0:nb] = s.bias_v[0:1, nb * d:nb * d + nb]
         buf[p, 0:1, nb:nb + ng] = s.gain_v[0:1, ng * d:ng * d + ng]
 
@@ -768,6 +823,8 @@
     if lined:
         s.spare = {D // GROUPS * 3: s.spare_wide, D // GROUPS: s.spare_tall, D: None}
     t.locate()
+    s.in_small[0:1, 0:nb] = s.in_bias[...].astype(f32).reshape(1, nb)
+    s.in_small[0:1, nb:nb + ng] = s.in_gain[...].astype(f32).reshape(1, ng)
 
     barrier = pltpu.get_barrier_semaphore()
     peers = t.peers()
@@ -782,7 +839,8 @@
                             [getattr(s, "g_" + k).at[i] for k in ("local", "s1", "r1", "s2", "r2", "s3", "r3")])
         scatter[n] = make[1](t, s.held[n], *[getattr(s, k + "_" + n) for k in ("ra", "rb", "rc")],
                              [getattr(s, "h_" + k).at[i] for k in ("s1", "r1", "s2", "r2", "s3", "r3")])
-    near_first = t.nx == 2
+    scatter["qkv"].halves = t.quads
+    near_first = t.near_first
     half = t.x if near_first else 0
     rest = 1 - half
 
@@ -798,8 +856,8 @@
     stage_mask(s)
     gather["small"].spread()
     gather["small"].share()
+    gather["out"].begin()
     gather["qkv"].spread()
-    gather["out"].begin()
     gather["up"].begin()
     gather["down"].begin()
     gather["small"].near_done()
@@ -817,24 +875,24 @@
     stage_attn_fwd(s, 3 * half + 1, 3 * half + 2)
     if near_first:
         gather["qkv"].share()
+    stage_attn_fwd(s, 3 * half + 2, 3 * half + 3)
     gather["up"].spread()
-    stage_attn_fwd(s, 3 * half + 2, 3 * half + 3)
-    gather["down"].spread()
+    gather["out"].share()
     if near_first:
         gather["qkv"].far_done()
     assemble_qkv(s, t, rest)
     stage_qkv(s, rest)
+    gather["down"].spread()
     stage_attn_fwd(s, 3 * rest, 3 * rest + 1)
-    gather["out"].share()
-    stage_attn_fwd(s, 3 * rest + 1, 3 * rest + 2)
     gather["out"].share_last()
     gather["up"].share()
+    stage_attn_fwd(s, 3 * rest + 1, 3 * rest + 2)
     stage_attn_fwd(s, 3 * rest + 2, 3 * rest + 3)
-    gather["down"].share()
     gather["out"].done()
     assemble(s, t, "out")
+    gather["down"].share()
+    stage_ln1(s)
     gather["up"].share_last()
-    stage_ln1(s)
     gather["down"].share_last()
     gather["up"].done()
     assemble(s, t, "up")
@@ -848,7 +906,7 @@
     give_out.start()
 
     def put(name):
-        return lambda g, v: lay_out(s, t, name, group_places(t, g, g // 2, g % 2), v)
+        return lambda g, v: lay_out(s, t, name, group_places(t, g, g // 2, g % 2, False), v)
 
     stage_down_grad(s, put("down"))
     scatter["down"].begin()
@@ -872,32 +930,43 @@
     scatter["up"].planes_last()
     stage_attn_back(s, 3 * rest + 2, 3 * rest + 3)
     scatter["down"].line()
-    put_qkv = lambda h: lambda g, i, v: lay_out(s, t, "qkv", group_places(t, g, h, i), v)
+    put_qkv = lambda h: lambda g, i, v: lay_out(s, t, "qkv", group_places(t, g, h, i, True), v)
     stage_qkv_grad(s, rest, put_qkv(rest))
     if near_first:
         scatter["qkv"].begin_far()
-    stage_attn_back(s, 3 * half, 3 * half + 1)
+    zh = t.z // 2 if t.quads else 0
+    first = 3 * half + (2 - 2 * zh if t.quads else 0)
+    last = 3 * half + (2 * zh if t.quads else 2)
+    stage_attn_back(s, first, first + 1)
     if near_first:
         scatter["qkv"].far()
     scatter["out"].planes_last()
     stage_attn_back(s, 3 * half + 1, 3 * half + 2)
+    if t.quads:
+        stage_qkv_grad_one(s, half, 1 - zh, put_qkv(half))
+        scatter["qkv"].begin_near(1)
     scatter["up"].line()
     s.grad_down[...] = scatter["down"].total()
-    stage_attn_back(s, 3 * half + 2, 3 * half + 3)
+    stage_attn_back(s, last, last + 1)
+    if t.quads:
+        scatter["qkv"].near(1)
+    lay_out_small(s, t)
+    scatter["small"].begin_far()
+    scatter["small"].begin_near(0)
     scatter["out"].line()
-    stage_qkv_grad(s, half, put_qkv(half))
+    if t.quads:
+        stage_qkv_grad_one(s, half, zh, put_qkv(half))
+    else:
+        stage_qkv_grad(s, half, put_qkv(half))
     if not near_first:
         scatter["qkv"].begin_far()
         scatter["qkv"].far()
-    scatter["qkv"].begin_near()
-    lay_out_small(s, t)
-    scatter["small"].begin_far()
-    scatter["small"].begin_near()
-    scatter["qkv"].near()
+    scatter["qkv"].begin_near(0)
     scatter["small"].far()
+    scatter["small"].near(0)
+    scatter["qkv"].near(0)
     stage_input_grad(s)
     give_din.start()
-    scatter["small"].near()
     s.grad_up[...] = scatter["up"].total()
     s.grad_out[...] = scatter["out"].total()
     s.grad_qkv[...] = scatter["qkv"].total()
@@ -938,7 +1007,7 @@
         blocks[n] = ((size // 128, 128) if lined else (size // group_shape[n][1], group_shape[n][1]), bf16)
     inputs = {
         "x_in": hidden_in[0], "seg": segment_ids, "pos": positions, "tok": token_mask, "cot_in": cotangent[0],
-        "in_small": jnp.concatenate([biases, gains]).astype(f32).reshape(1, nb + ng),
+        "in_bias": biases, "in_gain": gains,
         "in_qkv": qkv_weight.reshape(blocks["qkv"][0]),
         "in_out": out_weight.reshape(blocks["out"][0]),
         "in_up": up_weight.reshape(blocks["up"][0]),
@@ -958,7 +1027,7 @@
         dq=((T, D), bf16), dk=((T, D), bf16), dv=((T, D), bf16), joined=((GROUPS, T, 3 * gw), bf16),
         acc_g2=((8, D), f32), acc_s2=((8, D), f32), acc_down=((8, D), f32), acc_up=((8, FF), f32),
         acc_g1=((8, D), f32), acc_s1=((8, D), f32), acc_out=((8, D), f32),
-        bias_v=((1, nb * t.count), f32), gain_v=((1, ng * t.count), f32),
+        in_small=((1, nb + ng), f32), bias_v=((1, nb * t.count), f32), gain_v=((1, ng * t.count), f32),
         wqkv=((GROUPS, gw, 3 * gw), bf16), wout=((D, D), bf16), wup=((GROUPS, gw, fg), bf16),
         wdown=((GROUPS, fg, gw), bf16),
     )

time: 102 us -> 96.1 us (0.942)
  Pallas kernels: 99 us -> 95.1 us
  other arithmetic: 1.29 us -> 0 us
    pallas_call x1, Pallas kernels: 96 us -> 92 us  [body(): pl.pallas_call(lambda *refs: layer_kernel(names, t, (nb, ng), group_shape...]
    convert_element_type x1 -> x0, other arithmetic: 1.29 us -> none  [body(): jnp.concatenate([biases, gains]).astype(f32).reshape(1, nb + ng)]
where the time goes in v3:
time: 96.1 us; the launch traced here: 95.9 us
  Pallas kernels  95.1 us (99%)
    pallas_call x1, Pallas kernels, body(): pl.pallas_call(lambda *refs: layer_kernel(names, t, (nb, ng), group_shape...  92 us
    pallas_call x1, Pallas kernels, body(): pl.pallas_call(lambda *refs: hand_on(count, *refs), out_shape=[jax.ShapeD...  3.02 us

profile of v3, /device:TPU:0, one launch (start us, length us, event | category | flops | bytes accessed | tf_op | source)
XLA Modules:
  0.0 95.9 jit_solution(18427602209498061510)
XLA Ops:
  0.6 92.0 %layer.1 = (bf16[512,768]{1,0:T(8,128)(2,1)}, f32[512,768]{1,0:T(8,128)}, f32[108,128]{1,0:T(8,128)}, f32[144,128]{1,0:T(8,128)}, f32[144,128]{1,0:T(8,128)}, /*...) custom-call(bf16[512,768]{1,0:T(8,128)(2,1)} %bitcast.14, s32[1,512]{1,0:T(1,128)} %refs_1_.1, ...), custom_call_target="tpu_custom_call" | custom-call | tf_op jit(solution)/shard_map/layer/pallas_call | solution.py:1054
  92.7 3.0 %hand_on.1 = (bf16[512,768]{1,0:T(8,128)(2,1)}, f32[512,768]{1,0:T(8,128)}, f32[108,128]{1,0:T(8,128)}, f32[144,128]{1,0:T(8,128)}, f32[144,128]{1,0:T(8,128)}, ...) custom-call(bf16[512,768]{1,0:T(8,128)(2,1)} %get-tuple-element.24.refs_0_, ...), custom_call_target="tpu_custom_call" | custom-call | tf_op jit(solution)/shard_map/hand_on/pallas_call | solution.py:1066

commit v4 on v3

--- a/solution.py
+++ b/solution.py
@@ -84,7 +84,7 @@
 def stage_ln1(s):
     T, D = s.x.shape
     s.att[...] = dot(s.ctx[...], s.wout[...])
-    R = 32
+    R = 128
     def step(i, carry):
         rows = pl.ds(pl.multiple_of(i * R, R), R)
         u = s.x[rows, :].astype(f32) + (s.att[rows, :] + s.bias(2 * D, 0, D))
@@ -107,7 +107,7 @@
 def stage_ffn(s):
     T, D = s.x.shape
     gw, fg = D // GROUPS, FF // GROUPS
-    R = 128
+    R = 256
     def step(i, carry):
         rows = pl.ds(pl.multiple_of(i * R, R), R)
         for pair in range(2):
@@ -126,7 +126,7 @@
 
 def stage_ln2(s):
     T, D = s.x.shape
-    R = 32
+    R = 128
     for a in (s.acc_g2, s.acc_s2, s.acc_down):
         a[...] = jnp.zeros_like(a)
     def step(i, carry):
@@ -155,7 +155,7 @@
 def stage_ffn_back(s, lo, hi):
     T, D = s.x.shape
     gw, fg = D // GROUPS, FF // GROUPS
-    R = 128
+    R = 256
     if lo == 0:
         s.acc_up[...] = jnp.zeros_like(s.acc_up)
     def step(i, carry):
@@ -170,7 +170,7 @@
                 outs.append(dot_nt(di, s.wup[g]))
             s.att[rows, pair * 2 * gw:(pair + 1) * 2 * gw] = jnp.concatenate(outs, axis=1)
         return carry
-    lax.fori_loop(T // R * lo // 4, T // R * hi // 4, step, 0)
+    lax.fori_loop(T * lo // (4 * R), T * hi // (4 * R), step, 0)
 
 
 def stage_down_grad(s, put):
@@ -189,7 +189,7 @@
 
 def stage_ln1_back(s):
     T, D = s.x.shape
-    R = 32
+    R = 128
     for a in (s.acc_g1, s.acc_s1, s.acc_out):
         a[...] = jnp.zeros_like(a)
     def step(i, carry):
@@ -954,6 +954,7 @@
     scatter["small"].begin_far()
     scatter["small"].begin_near(0)
     scatter["out"].line()
+    scatter["small"].far()
     if t.quads:
         stage_qkv_grad_one(s, half, zh, put_qkv(half))
     else:
@@ -962,11 +963,10 @@
         scatter["qkv"].begin_far()
         scatter["qkv"].far()
     scatter["qkv"].begin_near(0)
-    scatter["small"].far()
-    scatter["small"].near(0)
-    scatter["qkv"].near(0)
     stage_input_grad(s)
     give_din.start()
+    scatter["qkv"].near(0)
+    scatter["small"].near(0)
     s.grad_up[...] = scatter["up"].total()
     s.grad_out[...] = scatter["out"].total()
     s.grad_qkv[...] = scatter["qkv"].total()

time: 96.1 us -> 88.6 us (0.922)
  Pallas kernels: 95.1 us -> 87.5 us
    pallas_call x1, Pallas kernels: 92 us -> 84.5 us  [body(): pl.pallas_call(lambda *refs: layer_kernel(names, t, (nb, ng), group_shape...]
where the time goes in v4:
time: 88.6 us; the launch traced here: 88.4 us
  Pallas kernels  87.5 us (99%)
    pallas_call x1, Pallas kernels, body(): pl.pallas_call(lambda *refs: layer_kernel(names, t, (nb, ng), group_shape...  84.5 us
    pallas_call x1, Pallas kernels, body(): pl.pallas_call(lambda *refs: hand_on(count, *refs), out_shape=[jax.ShapeD...  3.02 us

profile of v4, /device:TPU:0, one launch (start us, length us, event | category | flops | bytes accessed | tf_op | source)
XLA Modules:
  0.0 88.4 jit_solution(11566765586645222662)
XLA Ops:
  0.6 84.5 %layer.1 = (bf16[512,768]{1,0:T(8,128)(2,1)}, f32[512,768]{1,0:T(8,128)}, f32[108,128]{1,0:T(8,128)}, f32[144,128]{1,0:T(8,128)}, f32[144,128]{1,0:T(8,128)}, /*...) custom-call(bf16[512,768]{1,0:T(8,128)(2,1)} %bitcast.14, s32[1,512]{1,0:T(1,128)} %refs_1_.1, ...), custom_call_target="tpu_custom_call" | custom-call | tf_op jit(solution)/shard_map/layer/pallas_call | solution.py:1054
  85.2 3.0 %hand_on.1 = (bf16[512,768]{1,0:T(8,128)(2,1)}, f32[512,768]{1,0:T(8,128)}, f32[108,128]{1,0:T(8,128)}, f32[144,128]{1,0:T(8,128)}, f32[144,128]{1,0:T(8,128)}, ...) custom-call(bf16[512,768]{1,0:T(8,128)(2,1)} %get-tuple-element.24.refs_0_, ...), custom_call_target="tpu_custom_call" | custom-call | tf_op jit(solution)/shard_map/hand_on/pallas_call | solution.py:1066
